TPU v7x, 256 devices: a whole 4x4x8 slice. The times are simulated.
256 devices in a mesh: gx: 4 (over x), gy: 8 (over y, core), gz: 8 (over z).
Axes of the slice: x: 4, y: 4, z: 8, core: 2. Of those that a mesh axis runs over, the one named last changes fastest.
Arguments:
- residual_in: float32 [256, 512, 2048], P('gx', 'gy', 'gz'), may hold values from -700 to 700
Outputs:
- level_one: float32 [128, 256, 1024], P('gx', 'gy', 'gz')
- level_two: float32 [64, 128, 512], P('gx', 'gy', 'gz')
- level_three: float32 [32, 64, 256], P('gx', 'gy', 'gz')
- level_four: float32 [16, 32, 128], P('gx', 'gy', 'gz')
- level_five: float32 [8, 16, 64], P('gx', 'gy', 'gz')
- level_scales: float32 [5], replicated
All inputs are finite; a program needn't handle non-finite values.
Results may differ from a plain program's by a relative error of at most 0.0002.
Values sent between devices are 32-bit elements; how exact they have to be, the bound alone decides.
No kernel may reach another device: no remote copies, remote signals or barrier semaphores. Data moves between devices by JAX's collectives and lax.ppermute only.
A program may use at most 64 MiB of HBM per device.

v0:
```python
import functools

import jax
import jax.numpy as jnp
from jax import lax
from jax.sharding import Mesh
from jax.sharding import PartitionSpec as P

LEVELS = 5
GY = ("gy_0", "gy_1")
GX_GY_GZ = ("gx", "gy_0", "gy_1", "gz")


EPSILON = 1e-06


def shifted(block, axis, distance):
    devices = range(lax.axis_size(axis))
    route = [(i - distance, i) for i in devices if i - distance in devices]
    return lax.ppermute(block, axis, route)


def over_axes(array, axes):
    return functools.reduce(lax.psum, axes, array)


def pass_axis(values, axis_pos, rim_plane):
    length = values.shape[axis_pos]
    half = length // 2
    if axis_pos == 2:
        rows = lax.broadcasted_iota(jnp.int32, (length, half), 0)
        cols = lax.broadcasted_iota(jnp.int32, (length, half), 1)
        table = jnp.where(
            rows == 2 * cols,
            0.5,
            jnp.where((rows == 2 * cols + 1) | (rows == 2 * cols - 1), 0.25, 0.0),
        ).astype(jnp.float32)
        reduced = lax.dot_general(
            values,
            table,
            (((2,), (0,)), ((), ())),
            precision=lax.Precision.HIGHEST,
            preferred_element_type=jnp.float32,
        )
        tail = jnp.zeros(values.shape[:2] + (half - 1,), jnp.float32)
        return reduced + jnp.concatenate([0.25 * rim_plane, tail], axis=2)
    new_shape = values.shape[:axis_pos] + (half, 2) + values.shape[axis_pos + 1 :]
    paired = values.reshape(new_shape)
    even_part = lax.index_in_dim(paired, 0, axis_pos + 1, False)
    odd_part = lax.index_in_dim(paired, 1, axis_pos + 1, False)
    earlier = jnp.concatenate(
        [rim_plane, lax.slice_in_dim(odd_part, 0, half - 1, 1, axis_pos)], axis=axis_pos
    )
    return 0.5 * even_part + 0.25 * odd_part + 0.25 * earlier


def restrict_line(values, axis_pos):
    length = values.shape[axis_pos]
    last_plane = lax.slice_in_dim(values, length - 1, length, 1, axis_pos)
    if axis_pos == 0:
        rim_plane = shifted(last_plane, "gx", 1)
    elif axis_pos == 1:
        rim_plane = shifted(last_plane, GY, 1)
    else:
        rim_plane = shifted(last_plane, "gz", 1)
    return pass_axis(values, axis_pos, rim_plane)


def restrict_any(values):
    values = restrict_line(values, 0)
    values = restrict_line(values, 1)
    return restrict_line(values, 2)


def per_device(residual_in):
    devices_all = lax.axis_size("gx") * lax.axis_size(GY) * lax.axis_size("gz")
    current = residual_in
    grid_list = []
    scale_list = []
    unscaled = []
    sums_local = []
    for step_no in range(LEVELS):
        coarse = restrict_any(current)
        sums_local.append(jnp.sum(coarse * coarse))
        unscaled.append(coarse)
        current = coarse
    totals = over_axes(jnp.stack(sums_local), GX_GY_GZ)
    product = jnp.float32(1.0)
    for step_no in range(LEVELS):
        cells = unscaled[step_no].size * devices_all
        scale_now = jnp.sqrt(totals[step_no] / (product * product) / cells + EPSILON)
        product = product * scale_now
        grid_list.append(unscaled[step_no] / product)
        scale_list.append(scale_now)
    return (
        grid_list[0],
        grid_list[1],
        grid_list[2],
        grid_list[3],
        grid_list[4],
        jnp.stack(scale_list),
    )


def solution(mesh):
    torus = Mesh(
        mesh.devices.reshape(mesh.shape["gx"], 4, 2, mesh.shape["gz"]), ("gx", "gy_0", "gy_1", "gz")
    )
    placed = (P("gx", GY, "gz"),)
    return jax.shard_map(
        per_device,
        mesh=torus,
        in_specs=placed,
        out_specs=(
            P("gx", GY, "gz"),
            P("gx", GY, "gz"),
            P("gx", GY, "gz"),
            P("gx", GY, "gz"),
            P("gx", GY, "gz"),
            P(),
        ),
        check_vma=False,
    )
```

profile of v0, /device:TPU:1, one launch (start us, length us, event | category | flops | bytes accessed | tf_op | source)
XLA Modules:
  0.0 167.3 jit_solution(17785135824596561210)
XLA Ops:
  0.6 0.8 slice.172
  1.5 3.9 %collective-permute-start = (f32[1,64,256]{2,1,0:T(8,128)S(1)}, f32[1,64,256]{2,1,0:T(8,128)S(1)}, u32[]{:S(2)}, u32[]{:S(2)}) collective-permute-start(f32[1,64,256]{2,1,0:T(8,128)S(1)} %slice.172), channel_id=1, source_target_pairs={{0,64},{64,128},{128,192},{1,65},{65,129},{129,193},{2,66},{66,130... | collective-permute-start | bytes 196616 | tf_op jit(solution)/shard_map/ppermute | solution.py:20
  5.4 0.0 copy-start
  5.4 4.2 %slice_bitcast_fusion.2 = (f32[31,64,256]{2,1,0:T(8,128)}, f32[31,1,64,256]{3,2,0,1:T(8,128)}) fusion(f32[32,2,64,256]{3,2,1,0:T(8,128)} %bitcast.213), kind=kLoop, calls=%fused_computation.7 | loop fusion | bytes 6094848 | tf_op jit(solution)/shard_map/slice | solution.py:52
  9.7 0.4 fusion.1
  10.1 1.7 %fusion.116 = f32[32,64,256]{2,1,0:T(8,128)} fusion(f32[32,2,64,256]{3,2,1,0:T(8,128)S(1)} %bitcast.215), kind=kLoop, calls=%fused_computation.201 | loop fusion | flops 1572864 | bytes 6291456 | tf_op jit(solution)/shard_map/add | solution.py:54
  11.8 3.4 %concatenate.81 = f32[31,32,2,256]{3,2,1,0:T(2,128)} reshape(f32[31,1,64,256]{3,2,0,1:T(8,128)} %get-tuple-element.7) | data formatting | bytes 4063232 | tf_op jit(solution)/shard_map/concatenate | solution.py:51
  15.2 3.2 %copy.32 = f32[31,32,2,256]{3,1,0,2:T(8,128)} copy(f32[31,32,2,256]{3,2,1,0:T(2,128)} %concatenate.81) | data formatting | bytes 4063232 | tf_op jit(solution)/shard_map/concatenate | solution.py:51
  18.4 2.2 %add.185 = f32[32,32,2,256]{3,2,1,0:T(2,128)} reshape(f32[32,1,64,256]{3,2,0,1:T(8,128)S(1)} %fusion.1) | data formatting | bytes 4194304 | tf_op jit(solution)/shard_map/add | solution.py:54
  20.6 0.0 collective-permute-done
  20.7 1.2 slice_add_fusion
  21.9 4.0 %collective-permute-start.1 = (f32[32,1,256]{2,1,0:T(1,128)S(1)}, f32[32,1,256]{2,1,0:T(1,128)S(1)}, u32[]{:S(2)}, u32[]{:S(2)}) collective-permute-start(f32[32,1,256]{2,1,0:T(1,128)S(1)} %slice_add_fusion), channel_id=1, source_target_pairs={{0,8},{8,16},{16,24},{24,32},{32,40},{40,48},{48,56},{1,9},{9,17},... | collective-permute-start | bytes 98312 | tf_op jit(solution)/shard_map/ppermute | solution.py:20
  26.0 1.9 %fusion.3 = f32[32,32,2,256]{3,1,0,2:T(8,128)S(1)} fusion(f32[31,32,2,256]{3,1,0,2:T(8,128)} %copy.32, f32[1,32,2,256]{3,1,0,2:T(8,128)S(1)} %copy.31, f32[32,32,2,256]{3,2,1,0:T(2,128)S(1)} %copy-done.1), kind=kLoop, calls=%fused_computation.6 | loop fusion | flops 1572864 | bytes 6291456 | tf_op jit(solution)/shard_map/add | solution.py:54
  27.9 0.1 slice_bitcast_fusion.4
  28.1 0.4 fusion.6
  28.5 0.2 slice.232
  28.7 3.6 %collective-permute-start.2 = (f32[32,32,1]{2,1,0:T(8,128)S(1)}, f32[32,32,1]{2,1,0:T(8,128)S(1)}, u32[]{:S(2)}, u32[]{:S(2)}) collective-permute-start(f32[32,32,1]{2,1,0:T(8,128)S(1)} %slice.232), channel_id=1, source_target_pairs={{0,1},{1,2},{2,3},{3,4},{4,5},{5,6},{6,7},{8,9},{9,10},{10,11},{11... | collective-permute-start | bytes 12296 | tf_op jit(solution)/shard_map/ppermute | solution.py:20
  32.3 10.5 %collective-permute-done.2 = f32[32,32,1]{2,1,0:T(8,128)S(1)} collective-permute-done((f32[32,32,1]{2,1,0:T(8,128)S(1)}, f32[32,32,1]{2,1,0:T(8,128)S(1)}, u32[]{:S(2)}, u32[]{:S(2)}) %collective-permute-start.2) | collective-permute-done | bytes 4128 | tf_op jit(solution)/shard_map/ppermute | solution.py:20
  42.8 1.6 multiply_reduce_fusion
  44.5 3.1 %collective-permute-start.3 = (f32[1,32,128]{2,1,0:T(8,128)S(1)}, f32[1,32,128]{2,1,0:T(8,128)S(1)}, u32[]{:S(2)}, u32[]{:S(2)}) collective-permute-start(f32[1,32,128]{2,1,0:T(8,128)S(1)} %slice.235), channel_id=1, source_target_pairs={{0,64},{64,128},{128,192},{1,65},{65,129},{129,193},{2,66},{66,130... | collective-permute-start | bytes 49160 | tf_op jit(solution)/shard_map/ppermute | solution.py:20
  47.6 0.1 slice_bitcast_fusion.17
  47.7 0.8 collective-permute-done.3
  48.5 5.5 %collective-permute-start.4 = (f32[16,1,128]{2,1,0:T(1,128)S(1)}, f32[16,1,128]{2,1,0:T(1,128)S(1)}, u32[]{:S(2)}, u32[]{:S(2)}) collective-permute-start(f32[16,1,128]{2,1,0:T(1,128)S(1)} %slice_add_fusion.1), channel_id=1, source_target_pairs={{0,8},{8,16},{16,24},{24,32},{32,40},{40,48},{48,56},{1,9},{9,17},... | collective-permute-start | bytes 24584 | tf_op jit(solution)/shard_map/ppermute | solution.py:20
  54.1 0.7 collective-permute-done.4
  54.8 0.1 slice.241
  54.9 4.1 %collective-permute-start.5 = (f32[16,16,1]{2,1,0:T(8,128)S(1)}, f32[16,16,1]{2,1,0:T(8,128)S(1)}, u32[]{:S(2)}, u32[]{:S(2)}) collective-permute-start(f32[16,16,1]{2,1,0:T(8,128)S(1)} %slice.241), channel_id=1, source_target_pairs={{0,1},{1,2},{2,3},{3,4},{4,5},{5,6},{6,7},{8,9},{9,10},{10,11},{11... | collective-permute-start | bytes 3080 | tf_op jit(solution)/shard_map/ppermute | solution.py:20
  59.1 1.9 %collective-permute-done.5 = f32[16,16,1]{2,1,0:T(8,128)S(1)} collective-permute-done((f32[16,16,1]{2,1,0:T(8,128)S(1)}, f32[16,16,1]{2,1,0:T(8,128)S(1)}, u32[]{:S(2)}, u32[]{:S(2)}) %collective-permute-start.5) | collective-permute-done | bytes 1056 | tf_op jit(solution)/shard_map/ppermute | solution.py:20
  61.0 0.9 multiply_reduce_fusion.1
  62.0 3.9 %collective-permute-start.6 = (f32[1,16,64]{2,1,0:T(8,128)S(1)}, f32[1,16,64]{2,1,0:T(8,128)S(1)}, u32[]{:S(2)}, u32[]{:S(2)}) collective-permute-start(f32[1,16,64]{2,1,0:T(8,128)S(1)} %slice.244), channel_id=1, source_target_pairs={{0,64},{64,128},{128,192},{1,65},{65,129},{129,193},{2,66},{66,130... | collective-permute-start | bytes 12296 | tf_op jit(solution)/shard_map/ppermute | solution.py:20
  65.9 0.7 collective-permute-done.6
  66.7 5.9 %collective-permute-start.7 = (f32[8,1,64]{2,1,0:T(1,128)S(1)}, f32[8,1,64]{2,1,0:T(1,128)S(1)}, u32[]{:S(2)}, u32[]{:S(2)}) collective-permute-start(f32[8,1,64]{2,1,0:T(1,128)S(1)} %slice_add_fusion.2), channel_id=1, source_target_pairs={{0,8},{8,16},{16,24},{24,32},{32,40},{40,48},{48,56},{1,9},{9,17},... | collective-permute-start | bytes 6152 | tf_op jit(solution)/shard_map/ppermute | solution.py:20
  72.6 0.7 collective-permute-done.7
  73.4 0.1 slice.250
  73.4 4.1 %collective-permute-start.8 = (f32[8,8,1]{2,1,0:T(8,128)S(1)}, f32[8,8,1]{2,1,0:T(8,128)S(1)}, u32[]{:S(2)}, u32[]{:S(2)}) collective-permute-start(f32[8,8,1]{2,1,0:T(8,128)S(1)} %slice.250), channel_id=1, source_target_pairs={{0,1},{1,2},{2,3},{3,4},{4,5},{5,6},{6,7},{8,9},{9,10},{10,11},{11... | collective-permute-start | bytes 776 | tf_op jit(solution)/shard_map/ppermute | solution.py:20
  77.5 1.0 collective-permute-done.8
  78.5 0.8 multiply_reduce_fusion.2
  79.4 3.9 %collective-permute-start.9 = (f32[1,8,32]{2,1,0:T(8,128)S(1)}, f32[1,8,32]{2,1,0:T(8,128)S(1)}, u32[]{:S(2)}, u32[]{:S(2)}) collective-permute-start(f32[1,8,32]{2,1,0:T(8,128)S(1)} %slice.253), channel_id=1, source_target_pairs={{0,64},{64,128},{128,192},{1,65},{65,129},{129,193},{2,66},{66,130... | collective-permute-start | bytes 3080 | tf_op jit(solution)/shard_map/ppermute | solution.py:20
  83.3 0.7 collective-permute-done.9
  84.0 5.9 %collective-permute-start.10 = (f32[4,1,32]{2,1,0:T(1,128)S(1)}, f32[4,1,32]{2,1,0:T(1,128)S(1)}, u32[]{:S(2)}, u32[]{:S(2)}) collective-permute-start(f32[4,1,32]{2,1,0:T(1,128)S(1)} %slice_add_fusion.3), channel_id=1, source_target_pairs={{0,8},{8,16},{16,24},{24,32},{32,40},{40,48},{48,56},{1,9},{9,17},... | collective-permute-start | bytes 1544 | tf_op jit(solution)/shard_map/ppermute | solution.py:20
  90.0 0.7 collective-permute-done.10
  90.7 0.1 slice.259
  90.7 3.9 %collective-permute-start.11 = (f32[4,4,1]{2,1,0:T(4,128)S(1)}, f32[4,4,1]{2,1,0:T(4,128)S(1)}, u32[]{:S(2)}, u32[]{:S(2)}) collective-permute-start(f32[4,4,1]{2,1,0:T(4,128)S(1)} %slice.259), channel_id=1, source_target_pairs={{0,1},{1,2},{2,3},{3,4},{4,5},{5,6},{6,7},{8,9},{9,10},{10,11},{11... | collective-permute-start | bytes 200 | tf_op jit(solution)/shard_map/ppermute | solution.py:20
  94.7 0.8 collective-permute-done.11
  95.5 0.8 multiply_reduce_fusion.3
  96.3 3.9 %collective-permute-start.12 = (f32[1,4,16]{2,1,0:T(4,128)S(1)}, f32[1,4,16]{2,1,0:T(4,128)S(1)}, u32[]{:S(2)}, u32[]{:S(2)}) collective-permute-start(f32[1,4,16]{2,1,0:T(4,128)S(1)} %slice.262), channel_id=1, source_target_pairs={{0,64},{64,128},{128,192},{1,65},{65,129},{129,193},{2,66},{66,130... | collective-permute-start | bytes 776 | tf_op jit(solution)/shard_map/ppermute | solution.py:20
  100.2 0.7 collective-permute-done.12
  100.9 5.9 %collective-permute-start.13 = (f32[2,1,16]{2,1,0:T(1,128)S(1)}, f32[2,1,16]{2,1,0:T(1,128)S(1)}, u32[]{:S(2)}, u32[]{:S(2)}) collective-permute-start(f32[2,1,16]{2,1,0:T(1,128)S(1)} %slice_add_fusion.4), channel_id=1, source_target_pairs={{0,8},{8,16},{16,24},{24,32},{32,40},{40,48},{48,56},{1,9},{9,17},... | collective-permute-start | bytes 392 | tf_op jit(solution)/shard_map/ppermute | solution.py:20
  106.9 0.7 collective-permute-done.13
  107.5 0.1 slice.268
  107.6 5.0 %collective-permute-start.14 = (f32[2,2,1]{2,1,0:T(2,128)S(1)}, f32[2,2,1]{2,1,0:T(2,128)S(1)}, u32[]{:S(2)}, u32[]{:S(2)}) collective-permute-start(f32[2,2,1]{2,1,0:T(2,128)S(1)} %slice.268), channel_id=1, source_target_pairs={{0,1},{1,2},{2,3},{3,4},{4,5},{5,6},{6,7},{8,9},{9,10},{10,11},{11... | collective-permute-start | bytes 56 | tf_op jit(solution)/shard_map/ppermute | solution.py:20
  112.7 0.7 collective-permute-done.14
  113.4 0.8 multiply_reduce_fusion.4
  114.2 3.3 %stack.39 = f32[5]{0:T(128)S(1)} concatenate(f32[1]{0:T(128)} %bitcast.6, f32[1]{0:T(128)} %bitcast.16, f32[1]{0:T(128)} %bitcast.26, f32[1]{0:T(128)} %bitcast.36, f32[1]{0:T(128)} %bitcast.46), dimensions={0} | concatenate | bytes 40 | tf_op jit(solution)/shard_map/stack | solution.py:87
  117.5 8.0 %psum.28 = f32[5]{0:T(128)S(1)} all-reduce(f32[5]{0:T(128)S(1)} %stack.39), channel_id=1, replica_groups=mesh['gx'=4,'gy_0'=4,'gy_1'=2,'gz'=8] {'gx'}, use_global_device_ids=true, to_apply=%region_5.6 | all-reduce | flops 5 | bytes 40 | tf_op jit(solution)/shard_map/psum | solution.py:24
  125.5 7.0 %psum.29 = f32[5]{0:T(128)S(1)} all-reduce(f32[5]{0:T(128)S(1)} %psum.28), channel_id=1, replica_groups=mesh['gx'=4,'gy_0'=4,'gy_1'=2,'gz'=8] {'gy_0'}, use_global_device_ids=true, to_apply=%region_6.7 | all-reduce | flops 5 | bytes 40 | tf_op jit(solution)/shard_map/psum | solution.py:24
  132.5 8.4 %psum.30 = f32[5]{0:T(128)S(1)} all-reduce(f32[5]{0:T(128)S(1)} %psum.29), channel_id=1, replica_groups=mesh['gx'=4,'gy_0'=4,'gy_1'=2,'gz'=8] {'gy_1'}, use_global_device_ids=true, to_apply=%region_7.8 | all-reduce | flops 5 | bytes 40 | tf_op jit(solution)/shard_map/psum | solution.py:24
  140.8 18.4 %psum.31 = f32[5]{0:T(128)S(1)} all-reduce(f32[5]{0:T(128)S(1)} %psum.30), channel_id=1, replica_groups=mesh['gx'=4,'gy_0'=4,'gy_1'=2,'gz'=8] {'gz'}, use_global_device_ids=true, to_apply=%region_8.9 | all-reduce | flops 5 | bytes 40 | tf_op jit(solution)/shard_map/psum | solution.py:24
  159.3 0.6 fusion.106
  162.0 0.6 broadcast_divide_fusion.2
  162.6 0.7 broadcast_divide_fusion.1
  163.3 0.9 broadcast_divide_fusion
  165.6 0.6 broadcast_divide_fusion.3
  166.2 0.6 broadcast_divide_fusion.4
  166.7 0.6 stack.44
  (59 shorter events, 0.6 us)
Async XLA Ops:
  1.5 19.2 %collective-permute-start = (f32[1,64,256]{2,1,0:T(8,128)S(1)}, f32[1,64,256]{2,1,0:T(8,128)S(1)}, u32[]{:S(2)}, u32[]{:S(2)}) collective-permute-start(f32[1,64,256]{2,1,0:T(8,128)S(1)} %slice.172), channel_id=1, source_target_pairs={{0,64},{64,128},{128,192},{1,65},{65,129},{129,193},{2,66},{66,130... | collective-permute-start | bytes 196616 | tf_op jit(solution)/shard_map/ppermute | solution.py:20
  5.4 4.2 %copy-start = (f32[64,64,256]{2,1,0:T(8,128)S(1)}, f32[64,64,256]{2,1,0:T(8,128)}, u32[]{:S(2)}) copy-start(f32[64,64,256]{2,1,0:T(8,128)} %param.1) | copy-start | bytes 12582916
  20.6 5.4 %copy-start.1 = (f32[32,32,2,256]{3,2,1,0:T(2,128)S(1)}, f32[32,32,2,256]{3,2,1,0:T(2,128)}, u32[]{:S(2)}) copy-start(f32[32,32,2,256]{3,2,1,0:T(2,128)} %add.185) | copy-start | bytes 6291460
  21.9 6.1 %collective-permute-start.1 = (f32[32,1,256]{2,1,0:T(1,128)S(1)}, f32[32,1,256]{2,1,0:T(1,128)S(1)}, u32[]{:S(2)}, u32[]{:S(2)}) collective-permute-start(f32[32,1,256]{2,1,0:T(1,128)S(1)} %slice_add_fusion), channel_id=1, source_target_pairs={{0,8},{8,16},{16,24},{24,32},{32,40},{40,48},{48,56},{1,9},{9,17},... | collective-permute-start | bytes 98312 | tf_op jit(solution)/shard_map/ppermute | solution.py:20
  28.7 14.1 %collective-permute-start.2 = (f32[32,32,1]{2,1,0:T(8,128)S(1)}, f32[32,32,1]{2,1,0:T(8,128)S(1)}, u32[]{:S(2)}, u32[]{:S(2)}) collective-permute-start(f32[32,32,1]{2,1,0:T(8,128)S(1)} %slice.232), channel_id=1, source_target_pairs={{0,1},{1,2},{2,3},{3,4},{4,5},{5,6},{6,7},{8,9},{9,10},{10,11},{11... | collective-permute-start | bytes 12296 | tf_op jit(solution)/shard_map/ppermute | solution.py:20
  44.5 4.0 %collective-permute-start.3 = (f32[1,32,128]{2,1,0:T(8,128)S(1)}, f32[1,32,128]{2,1,0:T(8,128)S(1)}, u32[]{:S(2)}, u32[]{:S(2)}) collective-permute-start(f32[1,32,128]{2,1,0:T(8,128)S(1)} %slice.235), channel_id=1, source_target_pairs={{0,64},{64,128},{128,192},{1,65},{65,129},{129,193},{2,66},{66,130... | collective-permute-start | bytes 49160 | tf_op jit(solution)/shard_map/ppermute | solution.py:20
  48.5 6.3 %collective-permute-start.4 = (f32[16,1,128]{2,1,0:T(1,128)S(1)}, f32[16,1,128]{2,1,0:T(1,128)S(1)}, u32[]{:S(2)}, u32[]{:S(2)}) collective-permute-start(f32[16,1,128]{2,1,0:T(1,128)S(1)} %slice_add_fusion.1), channel_id=1, source_target_pairs={{0,8},{8,16},{16,24},{24,32},{32,40},{40,48},{48,56},{1,9},{9,17},... | collective-permute-start | bytes 24584 | tf_op jit(solution)/shard_map/ppermute | solution.py:20
  54.9 6.0 %collective-permute-start.5 = (f32[16,16,1]{2,1,0:T(8,128)S(1)}, f32[16,16,1]{2,1,0:T(8,128)S(1)}, u32[]{:S(2)}, u32[]{:S(2)}) collective-permute-start(f32[16,16,1]{2,1,0:T(8,128)S(1)} %slice.241), channel_id=1, source_target_pairs={{0,1},{1,2},{2,3},{3,4},{4,5},{5,6},{6,7},{8,9},{9,10},{10,11},{11... | collective-permute-start | bytes 3080 | tf_op jit(solution)/shard_map/ppermute | solution.py:20
  62.0 4.7 %collective-permute-start.6 = (f32[1,16,64]{2,1,0:T(8,128)S(1)}, f32[1,16,64]{2,1,0:T(8,128)S(1)}, u32[]{:S(2)}, u32[]{:S(2)}) collective-permute-start(f32[1,16,64]{2,1,0:T(8,128)S(1)} %slice.244), channel_id=1, source_target_pairs={{0,64},{64,128},{128,192},{1,65},{65,129},{129,193},{2,66},{66,130... | collective-permute-start | bytes 12296 | tf_op jit(solution)/shard_map/ppermute | solution.py:20
  66.7 6.6 %collective-permute-start.7 = (f32[8,1,64]{2,1,0:T(1,128)S(1)}, f32[8,1,64]{2,1,0:T(1,128)S(1)}, u32[]{:S(2)}, u32[]{:S(2)}) collective-permute-start(f32[8,1,64]{2,1,0:T(1,128)S(1)} %slice_add_fusion.2), channel_id=1, source_target_pairs={{0,8},{8,16},{16,24},{24,32},{32,40},{40,48},{48,56},{1,9},{9,17},... | collective-permute-start | bytes 6152 | tf_op jit(solution)/shard_map/ppermute | solution.py:20
  73.4 5.1 %collective-permute-start.8 = (f32[8,8,1]{2,1,0:T(8,128)S(1)}, f32[8,8,1]{2,1,0:T(8,128)S(1)}, u32[]{:S(2)}, u32[]{:S(2)}) collective-permute-start(f32[8,8,1]{2,1,0:T(8,128)S(1)} %slice.250), channel_id=1, source_target_pairs={{0,1},{1,2},{2,3},{3,4},{4,5},{5,6},{6,7},{8,9},{9,10},{10,11},{11... | collective-permute-start | bytes 776 | tf_op jit(solution)/shard_map/ppermute | solution.py:20
  79.4 4.7 %collective-permute-start.9 = (f32[1,8,32]{2,1,0:T(8,128)S(1)}, f32[1,8,32]{2,1,0:T(8,128)S(1)}, u32[]{:S(2)}, u32[]{:S(2)}) collective-permute-start(f32[1,8,32]{2,1,0:T(8,128)S(1)} %slice.253), channel_id=1, source_target_pairs={{0,64},{64,128},{128,192},{1,65},{65,129},{129,193},{2,66},{66,130... | collective-permute-start | bytes 3080 | tf_op jit(solution)/shard_map/ppermute | solution.py:20
  84.0 6.6 %collective-permute-start.10 = (f32[4,1,32]{2,1,0:T(1,128)S(1)}, f32[4,1,32]{2,1,0:T(1,128)S(1)}, u32[]{:S(2)}, u32[]{:S(2)}) collective-permute-start(f32[4,1,32]{2,1,0:T(1,128)S(1)} %slice_add_fusion.3), channel_id=1, source_target_pairs={{0,8},{8,16},{16,24},{24,32},{32,40},{40,48},{48,56},{1,9},{9,17},... | collective-permute-start | bytes 1544 | tf_op jit(solution)/shard_map/ppermute | solution.py:20
  90.7 4.7 %collective-permute-start.11 = (f32[4,4,1]{2,1,0:T(4,128)S(1)}, f32[4,4,1]{2,1,0:T(4,128)S(1)}, u32[]{:S(2)}, u32[]{:S(2)}) collective-permute-start(f32[4,4,1]{2,1,0:T(4,128)S(1)} %slice.259), channel_id=1, source_target_pairs={{0,1},{1,2},{2,3},{3,4},{4,5},{5,6},{6,7},{8,9},{9,10},{10,11},{11... | collective-permute-start | bytes 200 | tf_op jit(solution)/shard_map/ppermute | solution.py:20
  96.3 4.6 %collective-permute-start.12 = (f32[1,4,16]{2,1,0:T(4,128)S(1)}, f32[1,4,16]{2,1,0:T(4,128)S(1)}, u32[]{:S(2)}, u32[]{:S(2)}) collective-permute-start(f32[1,4,16]{2,1,0:T(4,128)S(1)} %slice.262), channel_id=1, source_target_pairs={{0,64},{64,128},{128,192},{1,65},{65,129},{129,193},{2,66},{66,130... | collective-permute-start | bytes 776 | tf_op jit(solution)/shard_map/ppermute | solution.py:20
  100.9 6.6 %collective-permute-start.13 = (f32[2,1,16]{2,1,0:T(1,128)S(1)}, f32[2,1,16]{2,1,0:T(1,128)S(1)}, u32[]{:S(2)}, u32[]{:S(2)}) collective-permute-start(f32[2,1,16]{2,1,0:T(1,128)S(1)} %slice_add_fusion.4), channel_id=1, source_target_pairs={{0,8},{8,16},{16,24},{24,32},{32,40},{40,48},{48,56},{1,9},{9,17},... | collective-permute-start | bytes 392 | tf_op jit(solution)/shard_map/ppermute | solution.py:20
  107.6 5.7 %collective-permute-start.14 = (f32[2,2,1]{2,1,0:T(2,128)S(1)}, f32[2,2,1]{2,1,0:T(2,128)S(1)}, u32[]{:S(2)}, u32[]{:S(2)}) collective-permute-start(f32[2,2,1]{2,1,0:T(2,128)S(1)} %slice.268), channel_id=1, source_target_pairs={{0,1},{1,2},{2,3},{3,4},{4,5},{5,6},{6,7},{8,9},{9,10},{10,11},{11... | collective-permute-start | bytes 56 | tf_op jit(solution)/shard_map/ppermute | solution.py:20
where the time goes:
time: 170 us; the launch traced here: 167 us
  starting transfers between devices  66.7 us (39%)
  blocking collectives  41.8 us (25%)
  waiting for transfers between devices  20.6 us (12%)
  local copies, waits for them, and re-layouts  19.2 us (11%)
  other arithmetic  9.44 us (6%)
  matrix products  5.04 us (3%)
  between operations  4.58 us (3%)
    ppermute x15, starting transfers between devices, shifted(): return lax.ppermute(block, axis, route)  66.7 us
    psum x4, blocking collectives, over_axes(): return functools.reduce(lax.psum, axes, array)  41.8 us
    ppermute x15, waiting for transfers between devices, shifted(): return lax.ppermute(block, axis, route)  20.6 us
    concatenate x10, local copies, waits for them, and re-layouts, pass_axis(): jnp.concatenate([rim_plane, lax.slice_in_dim(odd_part, 0, half - 1, 1, ax...  6.7 us
    add x25, other arithmetic, pass_axis(): return 0.5 * even_part + 0.25 * odd_part + 0.25 * earlier  5.99 us
    dot_general x5, matrix products, pass_axis(): lax.dot_general(values, table, (((2,), (0,)), ((), ())), precision=lax.Pr...  5.04 us
    slice x6, local copies, waits for them, and re-layouts, pass_axis(): lax.slice_in_dim(odd_part, 0, half - 1, 1, axis_pos)  4.3 us
  transfers between devices with their start and end apart: 15, of which 13 were waited for; matrix products, arithmetic and copies ran while one was open for 10% of the time, Pallas kernels for 0%

commit v1 on v0

v1 whole, which is shorter than its diff:
```python
import jax
import jax.numpy as jnp
from jax import lax
from jax.experimental import pallas as pl
from jax.experimental.pallas import tpu as pltpu
from jax.sharding import Mesh
from jax.sharding import PartitionSpec as P

LEVELS = 5
GY = ("gy_0", "gy_1")
GX_GY_GZ = ("gx", "gy_0", "gy_1", "gz")
EPSILON = 1e-06

BX, BY, BZ = 64, 64, 256
LANES = 128
CHUNK = 8
COUNT = [BX >> level for level in range(1, LEVELS + 1)]
ROWS = [40, 24, 16, 8, 8]
PASS_ROWS = [88, 56, 40, 24, 24]
REST_AT = [0, 0, 408, 552, 592]
REST_ROWS = 616
FIRST_ROWS = (COUNT[0] + 1) * ROWS[0]
LANE_AT = [0, 0, 64, 96, 112]
LANE_COUNT = [128, 64, 32, 16, 8]
END_AT = 120
FACE_AT = [-1, 30, 45, 52, 55]


def face_lane(level, plane):
    return END_AT + level if plane == 0 else FACE_AT[level] + plane


def iota(shape, dim):
    return lax.broadcasted_iota(jnp.int32, shape, dim)


def tile_mask(level, shape):
    lane = iota(shape, len(shape) - 1)
    return (lane >= LANE_AT[level]) & (lane < LANE_AT[level] + LANE_COUNT[level])


def face_mask(level, shape):
    lane = iota(shape, len(shape) - 1)
    first = FACE_AT[level] + 1
    return (lane == END_AT + level) | ((lane >= first) & (lane < first + COUNT[level] - 1))


def stencil_table():
    lane = iota((1, BZ), 1)
    width = jnp.zeros((1, BZ), jnp.float32)
    centre = jnp.zeros((1, BZ), jnp.float32)
    scale = jnp.zeros((1, BZ), jnp.float32)
    for level in range(LEVELS):
        step = 2 << level
        base = LANE_AT[level] + (LANES if level else 0)
        inside = (lane >= base) & (lane < base + LANE_COUNT[level])
        past = lane == LANES + END_AT + level
        width = jnp.where(inside | past, float(step), width)
        scale = jnp.where(inside | past, 1.0 / 64 ** (level + 1), scale)
        centre = jnp.where(inside, ((lane - base) * step).astype(jnp.float32), centre)
        centre = jnp.where(past, float(BZ), centre)
    row = iota((BZ, BZ), 0).astype(jnp.float32)
    return (jnp.maximum(width - jnp.abs(row - centre), 0.0) * scale).astype(jnp.bfloat16)


def apply_table(values, table):
    high = values.astype(jnp.bfloat16)
    low = (values - high.astype(jnp.float32)).astype(jnp.bfloat16)
    top = jnp.dot(high, table, preferred_element_type=jnp.float32)
    return top + jnp.dot(low, table, preferred_element_type=jnp.float32)


def aligned(start):
    return start if isinstance(start, int) else pl.multiple_of(start, 8)


def y_pass(pass_ref, plane, level):
    base = aligned(plane * PASS_ROWS[level]) + 8
    full = (COUNT[level] // 8) * 8
    parts = []
    if full:
        middle = pass_ref[pl.ds(base, full, stride=2), :]
        after = pass_ref[pl.ds(base + 1, full, stride=2), :]
        before = pass_ref[pl.ds(base - 1, full, stride=2), :]
        parts.append(before + after + (middle + middle))
    rest = ROWS[level] - full
    before = pass_ref[pl.ds(base + 2 * full - 1, rest, stride=2), :]
    if level:
        middle = pass_ref[pl.ds(base + 2 * full, rest, stride=2), :]
        before += middle + middle
    if not full:
        before += pass_ref[pl.ds(base + 1, rest, stride=2), :]
    parts.append(before)
    return parts[0] if len(parts) == 1 else jnp.concatenate(parts, axis=0)


def local_kernel(grid_ref, first_ref, rest_ref, xface_ref, yface_ref, zface_ref, *scratch):
    block_ref, plane_ref, stack_ref, end_ref, sems = scratch[:5]
    pass_refs = [scratch[5 + 2 * level : 7 + 2 * level] for level in range(LEVELS)]

    def chunk_copy(index):
        return pltpu.make_async_copy(
            grid_ref.at[pl.ds(index * CHUNK, CHUNK)],
            block_ref.at[pl.ds(index * CHUNK + 1, CHUNK)],
            sems.at[index],
        )

    chunks = BX // CHUNK
    for index in range(chunks):
        chunk_copy(index).start()
    table = stencil_table()
    block_ref[0] = jnp.zeros((BY, BZ), jnp.float32)
    for level in range(LEVELS):
        body = BY if level == 0 else ROWS[level - 1]
        tail = PASS_ROWS[level] - 8 - body
        for half in range(2):
            ref = pass_refs[level][half]
            for plane in range(COUNT[level] + 1):
                base = plane * PASS_ROWS[level]
                ref[pl.ds(base, 8), :] = jnp.zeros((8, LANES), jnp.float32)
                if tail:
                    ref[pl.ds(base + 8 + body, tail), :] = jnp.zeros((tail, LANES), jnp.float32)

    def first_y(plane):
        for half in range(2):
            lanes = slice(half * LANES, (half + 1) * LANES)
            out = y_pass(pass_refs[0][half], plane, 0)
            plane_ref[pl.ds(aligned(plane * ROWS[0]), ROWS[0]), lanes] = out

    def first_level(index, carry):
        chunk_copy(index).wait()
        for part in range(CHUNK // 2):
            plane = index * (CHUNK // 2) + part
            for half in range(2):
                lanes = slice(half * LANES, (half + 1) * LANES)
                before = block_ref[2 * plane, :, lanes]
                middle = block_ref[2 * plane + 1, :, lanes]
                after = block_ref[2 * plane + 2, :, lanes]
                pass_refs[0][half][pl.ds(aligned(plane * PASS_ROWS[0]) + 8, BY), :] = (
                    before + after + (middle + middle)
                )
        for part in range(CHUNK // 2):
            first_y(index * (CHUNK // 2) + part)
        return carry

    lax.fori_loop(0, chunks, first_level, 0)
    for half in range(2):
        lanes = slice(half * LANES, (half + 1) * LANES)
        pass_refs[0][half][pl.ds(COUNT[0] * PASS_ROWS[0] + 8, BY), :] = block_ref[BX, :, lanes]
    first_y(COUNT[0])

    for level in range(1, LEVELS):
        source = plane_ref if level == 1 else stack_ref
        source_at = REST_AT[level - 1] if level > 1 else 0
        rows = ROWS[level - 1]
        for half in range(2):
            lanes = slice(half * LANES, (half + 1) * LANES)
            ref = pass_refs[level][half]
            for plane in range(COUNT[level] + 1):
                middle = source[pl.ds(source_at + 2 * plane * rows, rows), lanes]
                total = middle + middle
                if plane > 0:
                    total += source[pl.ds(source_at + (2 * plane - 1) * rows, rows), lanes]
                if plane < COUNT[level]:
                    total += source[pl.ds(source_at + (2 * plane + 1) * rows, rows), lanes]
                ref[pl.ds(plane * PASS_ROWS[level] + 8, rows), :] = total
            for plane in range(COUNT[level] + 1):
                at = REST_AT[level] + plane * ROWS[level]
                stack_ref[pl.ds(at, ROWS[level]), lanes] = y_pass(ref, plane, level)

    span = 8 * ROWS[0]

    def first_z(index, carry):
        at = aligned(index * span)
        both = apply_table(plane_ref[pl.ds(at, span), :], table)
        first_ref[pl.ds(at, span), :] = both[:, :LANES]
        end_ref[pl.ds(at, span), :] = both[:, LANES:]
        return carry

    lax.fori_loop(0, COUNT[0] // 8, first_z, 0)
    last = COUNT[0] * ROWS[0]
    both = apply_table(plane_ref[pl.ds(last, ROWS[0]), :], table)
    first_ref[pl.ds(last, ROWS[0]), :] = both[:, :LANES]
    end_ref[pl.ds(last, ROWS[0]), :] = both[:, LANES:]
    rest_ref[...] = apply_table(stack_ref[...], table[:, LANES:])

    def right_rows(level, plane):
        ref = end_ref if level == 0 else rest_ref
        at = (0 if level == 0 else REST_AT[level]) + plane * ROWS[level]
        return ref[pl.ds(at, ROWS[level]), :]

    xface_ref[:, :LANES] = first_ref[pl.ds(last, ROWS[0]), :]
    tile = jnp.where(iota((ROWS[0], LANES), 1) == END_AT, right_rows(0, COUNT[0]), 0.0)
    xface_ref[:, LANES:] = tile
    for level in range(1, LEVELS):
        shape = (ROWS[level], LANES)
        keep = tile_mask(level, shape) | (iota(shape, 1) == END_AT + level)
        old = xface_ref[pl.ds(0, ROWS[level]), LANES:]
        xface_ref[pl.ds(0, ROWS[level]), LANES:] = jnp.where(keep, right_rows(level, COUNT[level]), old)

    yface_ref[:, :LANES] = first_ref[pl.ds(COUNT[0], COUNT[0], stride=ROWS[0]), :]
    yface_ref[:, LANES:] = jnp.zeros((COUNT[0], LANES), jnp.float32)
    for level in range(1, LEVELS):
        count = COUNT[level]
        at = REST_AT[level] + count
        if count >= 8:
            new = rest_ref[pl.ds(at, count, stride=ROWS[level]), :]
        else:
            new = jnp.zeros((8, LANES), jnp.float32)
            for plane in range(count):
                row = rest_ref[pl.ds(at + plane * ROWS[level], 1), :]
                new = jnp.where(iota((8, LANES), 0) == plane, row, new)
        size = max(count, 8)
        old = yface_ref[pl.ds(0, size), LANES:]
        yface_ref[pl.ds(0, size), LANES:] = jnp.where(tile_mask(level, (size, LANES)), new, old)

    total = None
    for level in range(LEVELS):
        lane = iota((ROWS[level], LANES), 1)
        face = jnp.zeros((ROWS[level], LANES), jnp.float32)
        for plane in range(COUNT[level]):
            values = right_rows(level, plane)
            target = face_lane(level, plane)
            shift = (target - END_AT - level) % LANES
            if shift:
                values = pltpu.roll(values, shift, 1)
            face = jnp.where(lane == target, values, face)
        if total is None:
            zface_ref[...] = face
            total = True
        else:
            zface_ref[pl.ds(0, ROWS[level]), :] = zface_ref[pl.ds(0, ROWS[level]), :] + face


def local_restriction(block):
    f32 = jnp.float32
    scratch = [
        pltpu.VMEM((BX + 1, BY, BZ), f32),
        pltpu.VMEM((FIRST_ROWS, BZ), f32),
        pltpu.VMEM((REST_ROWS, BZ), f32),
        pltpu.VMEM((FIRST_ROWS, LANES), f32),
        pltpu.SemaphoreType.DMA((BX // CHUNK,)),
    ]
    for level in range(LEVELS):
        shape = ((COUNT[level] + 1) * PASS_ROWS[level], LANES)
        scratch += [pltpu.VMEM(shape, f32), pltpu.VMEM(shape, f32)]
    vmem = pl.BlockSpec(memory_space=pltpu.VMEM)
    return pl.pallas_call(
        local_kernel,
        out_shape=(
            jax.ShapeDtypeStruct((FIRST_ROWS, LANES), f32),
            jax.ShapeDtypeStruct((REST_ROWS, LANES), f32),
            jax.ShapeDtypeStruct((ROWS[0], BZ), f32),
            jax.ShapeDtypeStruct((COUNT[0], BZ), f32),
            jax.ShapeDtypeStruct((ROWS[0], LANES), f32),
        ),
        in_specs=[pl.BlockSpec(memory_space=pl.ANY)],
        out_specs=(vmem,) * 5,
        scratch_shapes=scratch,
        name="local_levels",
    )(block)


def edge_kernel(xin_ref, yface_ref, zface_ref, yout_ref, zout_ref):
    count = COUNT[0]
    lane = iota((ROWS[0], LANES), 1)
    zface = zface_ref[...] + jnp.where(lane >= END_AT, xin_ref[:, LANES:], 0.0)
    zout_ref[...] = zface
    row = iota((count, LANES), 0)
    yout_ref[pl.ds(0, count), :LANES] = yface_ref[:, :LANES] + jnp.where(
        row == 0, xin_ref[pl.ds(count, 1), :LANES], 0.0
    )
    edge = jnp.zeros((1, LANES), jnp.float32)
    corner = jnp.zeros((1, LANES), jnp.float32)
    for level in range(LEVELS):
        at = pl.ds(COUNT[level], 1)
        if level:
            edge = jnp.where(tile_mask(level, (1, LANES)), xin_ref[at, LANES:], edge)
        corner = jnp.where(face_mask(level, (1, LANES)), zout_ref[at, :], corner)
    yout_ref[pl.ds(0, count), LANES:] = yface_ref[:, LANES:] + jnp.where(row == 0, edge, 0.0)
    yout_ref[pl.ds(count, 8), :LANES] = jnp.where(iota((8, LANES), 0) == 0, corner, 0.0)
    yout_ref[pl.ds(count, 8), LANES:] = jnp.zeros((8, LANES), jnp.float32)


def add_edges(xin, yface, zface):
    f32 = jnp.float32
    vmem = pl.BlockSpec(memory_space=pltpu.VMEM)
    return pl.pallas_call(
        edge_kernel,
        out_shape=(
            jax.ShapeDtypeStruct((ROWS[0], BZ), f32),
            jax.ShapeDtypeStruct((ROWS[0], LANES), f32),
        ),
        in_specs=[vmem] * 3,
        out_specs=(vmem,) * 2,
        name="edges",
    )(xin, yface, zface)


def finish_kernel(first_ref, rest_ref, xin_ref, yin_ref, zin_ref, *out_refs):
    sums_ref = out_refs[LEVELS]
    sums = jnp.zeros((1, LANES), jnp.float32)
    for level in range(LEVELS):
        count = COUNT[level]
        rows = max(count, 8)
        half = slice(0, LANES) if level == 0 else slice(LANES, 2 * LANES)
        source = first_ref if level == 0 else rest_ref
        shape = (rows, LANES)
        inside = tile_mask(level, shape) & (iota(shape, 0) < count)
        zlane = iota(shape, 1) == LANE_AT[level]
        squares = jnp.zeros((8, LANES), jnp.float32)
        for plane in range(count):
            at = REST_AT[level] + plane * ROWS[level]
            values = source[pl.ds(at, rows), :]
            if plane == 0:
                values = values + xin_ref[pl.ds(0, rows), half]
            yrow = jnp.where(iota((8, LANES), 0) == 0, yin_ref[pl.ds(plane, 1), half], 0.0)
            if rows > 8:
                yrow = jnp.concatenate([yrow, jnp.zeros((rows - 8, LANES), jnp.float32)], axis=0)
            shift = (LANE_AT[level] - face_lane(level, plane)) % LANES
            zcol = zin_ref[pl.ds(0, rows), :]
            if shift:
                zcol = pltpu.roll(zcol, shift, 1)
            values = values + yrow + jnp.where(zlane, zcol, 0.0)
            if level:
                values = jnp.where(inside, values, 0.0)
            out_refs[level][plane] = values
            squared = values * values
            for tile in range(rows // 8):
                squares = squares + squared[tile * 8 : tile * 8 + 8]
        total = jnp.sum(jnp.sum(squares, axis=0, keepdims=True), axis=1, keepdims=True)
        sums = jnp.where(iota((1, LANES), 1) == level, total, sums)
    sums_ref[...] = jnp.broadcast_to(sums, sums_ref.shape)


def finish_levels(first, rest, xin, yin, zin, devices):
    f32 = jnp.float32
    vmem = pl.BlockSpec(memory_space=pltpu.VMEM)
    shapes = [(COUNT[level], max(COUNT[level], 8), LANES) for level in range(LEVELS)]
    shapes.append((devices, LANES))
    return pl.pallas_call(
        finish_kernel,
        out_shape=tuple(jax.ShapeDtypeStruct(shape, f32) for shape in shapes),
        in_specs=[vmem] * 5,
        out_specs=(vmem,) * 6,
        name="finish",
    )(first, rest, xin, yin, zin)


def scale_kernel(sums_ref, *refs):
    level_refs = refs[:LEVELS]
    out_refs = refs[LEVELS : 2 * LEVELS]
    scales_ref = refs[2 * LEVELS]
    devices = sums_ref.shape[0]
    totals = jnp.sum(sums_ref[...], axis=0, keepdims=True)
    lane = iota((1, LANES), 1)
    product = jnp.ones((1, 1), jnp.float32)
    scales = jnp.zeros((1, LANES), jnp.float32)
    for level in range(LEVELS):
        cells = COUNT[level] * COUNT[level] * LANE_COUNT[level] * devices
        total = jnp.sum(jnp.where(lane == level, totals, 0.0), axis=1, keepdims=True)
        scale = jnp.sqrt(total / (product * product) * (1.0 / cells) + EPSILON)
        product = product * scale
        scales = jnp.where(lane == level, scale, scales)
        factor = jnp.broadcast_to(1.0 / product, (8, LANES))
        count = COUNT[level]
        for plane in range(count):
            for tile in range(max(count // 8, 1)):
                values = level_refs[level][plane, pl.ds(tile * 8, 8), :] * factor
                if LANE_AT[level]:
                    values = pltpu.roll(values, LANES - LANE_AT[level], 1)
                size = min(count, 8)
                out_refs[level][plane, pl.ds(tile * 8, size), :] = values[:size, : LANE_COUNT[level]]
    scales_ref[...] = scales[0, :LEVELS]


def scale_levels(sums, levels):
    f32 = jnp.float32
    vmem = pl.BlockSpec(memory_space=pltpu.VMEM)
    shapes = [(COUNT[level], COUNT[level], LANE_COUNT[level]) for level in range(LEVELS)]
    shapes.append((LEVELS,))
    return pl.pallas_call(
        scale_kernel,
        out_shape=tuple(jax.ShapeDtypeStruct(shape, f32) for shape in shapes),
        in_specs=[vmem] * 6,
        out_specs=(vmem,) * 6,
        name="scale",
    )(sums, *levels)


def to_next(face, axis):
    return lax.ppermute(face, axis, [(i, i + 1) for i in range(lax.axis_size(axis) - 1)])


def per_device(residual_in):
    devices = lax.axis_size(GX_GY_GZ)
    first, rest, xface, yface, zface = local_restriction(residual_in)
    xin = to_next(xface, "gx")
    yface, zface = add_edges(xin, yface, zface)
    yin = to_next(yface, GY)
    corner = jnp.where(iota((COUNT[0], LANES), 0) == 0, yin[COUNT[0], :LANES], 0.0)
    zin = to_next(zface[: COUNT[0]] + corner, "gz")
    *levels, sums = finish_levels(first, rest, xin, yin, zin, devices)
    sums = lax.all_to_all(sums, GX_GY_GZ, 0, 0, tiled=True)
    return tuple(scale_levels(sums, levels))


def solution(mesh):
    torus = Mesh(
        mesh.devices.reshape(mesh.shape["gx"], mesh.shape["gy"] // 2, 2, mesh.shape["gz"]), GX_GY_GZ
    )
    placed = P("gx", GY, "gz")
    return jax.shard_map(
        per_device,
        mesh=torus,
        in_specs=(placed,),
        out_specs=(placed,) * LEVELS + (P(),),
        check_vma=False,
    )
```

time: 170 us -> 61.2 us (0.36); the launches traced: 167 us -> 60.9 us
  starting transfers between devices: 66.7 us -> 12.1 us
  local copies, waits for them, and re-layouts: 19.2 us -> 1.22 us
  waiting for transfers between devices: 20.6 us -> 3.63 us
  Pallas kernels: 0 us -> 10.7 us
  blocking collectives: 41.8 us -> 31.7 us
  other arithmetic: 9.44 us -> 0.81 us
  matrix products: 5.04 us -> 0 us
  between operations: 4.58 us -> 0.68 us
    ppermute x15 -> x3, starting transfers between devices: 66.7 us -> 12.1 us  [to_next(): lax.ppermute(face, axis, [(i, i + 1) for i in range(lax.axis_size(axis) -...]
    psum x4 -> x0, blocking collectives: 41.8 us -> none  [over_axes(): return functools.reduce(lax.psum, axes, array)]
    all_to_all x0 -> x1, blocking collectives: none -> 31.7 us  [per_device(): sums = lax.all_to_all(sums, GX_GY_GZ, 0, 0, tiled=True)]
    ppermute x15 -> x3, waiting for transfers between devices: 20.6 us -> 3.63 us  [to_next(): lax.ppermute(face, axis, [(i, i + 1) for i in range(lax.axis_size(axis) -...]
    pallas_call x0 -> x4, Pallas kernels: none -> 10.7 us  [the longest x1 4.81 us: local_restriction(): pl.pallas_call(local_kernel, out_shape=(jax.ShapeDtypeStruct((FIRST_ROWS,...]
    concatenate x10 -> x0, local copies, waits for them, and re-layouts: 6.7 us -> none  [pass_axis(): jnp.concatenate([rim_plane, lax.slice_in_dim(odd_part, 0, half - 1, 1, ax...]
    slice x17 -> x0, local copies, waits for them, and re-layouts: 6.26 us -> none  [the longest x6 4.3 us: pass_axis(): lax.slice_in_dim(odd_part, 0, half - 1, 1, axis_pos)]
    add x30 -> x1, other arithmetic: 6.01 us -> 0.8 us  [per_device(): zin = to_next(zface[:COUNT[0]] + corner, 'gz')]
  transfers between devices with their start and end apart: 15 -> 3, of which waited for: 13 -> 3; matrix products, arithmetic and copies ran while one was open for 10% -> 0% of each run, Pallas kernels for 0% -> 0%
where the time goes in v1:
time: 61.2 us; the launch traced here: 60.9 us
  blocking collectives  31.7 us (52%)
  starting transfers between devices  12.1 us (20%)
  Pallas kernels  10.7 us (17%)
  waiting for transfers between devices  3.63 us (6%)
  local copies, waits for them, and re-layouts  1.22 us (2%)
  other arithmetic  0.81 us (1%)
  between operations  0.68 us (1%)
    all_to_all x1, blocking collectives, per_device(): sums = lax.all_to_all(sums, GX_GY_GZ, 0, 0, tiled=True)  31.7 us
    ppermute x3, starting transfers between devices, to_next(): lax.ppermute(face, axis, [(i, i + 1) for i in range(lax.axis_size(axis) -...  12.1 us
    pallas_call x1, Pallas kernels, local_restriction(): pl.pallas_call(local_kernel, out_shape=(jax.ShapeDtypeStruct((FIRST_ROWS,...  4.81 us
    ppermute x3, waiting for transfers between devices, to_next(): lax.ppermute(face, axis, [(i, i + 1) for i in range(lax.axis_size(axis) -...  3.63 us
    pallas_call x1, Pallas kernels, finish_levels(): pl.pallas_call(finish_kernel, out_shape=tuple((jax.ShapeDtypeStruct(shape...  2.37 us
    pallas_call x1, Pallas kernels, scale_levels(): pl.pallas_call(scale_kernel, out_shape=tuple((jax.ShapeDtypeStruct(shape,...  2.13 us
    pallas_call x1, Pallas kernels, add_edges(): pl.pallas_call(edge_kernel, out_shape=(jax.ShapeDtypeStruct((ROWS[0], BZ)...  1.44 us
  transfers between devices with their start and end apart: 3, of which 3 were waited for; matrix products, arithmetic and copies ran while one was open for 0% of the time, Pallas kernels for 0%

profile of v1, /device:TPU:1, one launch (start us, length us, event | category | flops | bytes accessed | tf_op | source)
XLA Modules:
  0.0 60.9 jit_solution(8585535900431772920)
XLA Ops:
  0.6 4.8 %local_levels.1 = (f32[1320,128]{1,0:T(8,128)}, f32[616,128]{1,0:T(8,128)}, f32[40,256]{1,0:T(8,128)}, f32[32,256]{1,0:T(8,128)}, f32[40,128]{1,0:T(8,128)}) custom-call(f32[64,64,256]{2,1,0:T(8,128)} %grid_ref.1), custom_call_target="tpu_custom_call" | custom-call | tf_op jit(solution)/shard_map/local_levels/pallas_call | solution.py:248
  5.4 3.9 %collective-permute-start = (f32[40,256]{1,0:T(8,128)}, f32[40,256]{1,0:T(8,128)S(1)}, u32[]{:S(2)}, u32[]{:S(2)}) collective-permute-start(f32[40,256]{1,0:T(8,128)} %get-tuple-element.21), channel_id=1, source_target_pairs={{0,64},{64,128},{128,192},{1,65},{65,129},{129,193},{2,66},{66,130... | collective-permute-start | bytes 122888 | tf_op jit(solution)/shard_map/ppermute | solution.py:392
  9.4 1.4 %collective-permute-done.xin_ref = f32[40,256]{1,0:T(8,128)S(1)} collective-permute-done((f32[40,256]{1,0:T(8,128)}, f32[40,256]{1,0:T(8,128)S(1)}, u32[]{:S(2)}, u32[]{:S(2)}) %collective-permute-start) | collective-permute-done | bytes 40992 | tf_op jit(solution)/shard_map/ppermute | solution.py:392
  10.8 0.0 copy-start
  10.8 0.6 %copy-done = f32[40,256]{1,0:T(8,128)} copy-done((f32[40,256]{1,0:T(8,128)}, f32[40,256]{1,0:T(8,128)S(1)}, u32[]{:S(2)}) %copy-start) | copy-done | bytes 40984
  11.4 1.4 %edges.1 = (f32[40,256]{1,0:T(8,128)}, f32[40,128]{1,0:T(8,128)}) custom-call(f32[40,256]{1,0:T(8,128)} %copy-done, f32[32,256]{1,0:T(8,128)} %get-tuple-element.22.yface_ref, f32[40,128]{1,0:T(8,128)} %get-tuple-element.23.zface_ref), custom_call_target="tpu_custom_call" | custom-call | tf_op jit(solution)/shard_map/edges/pallas_call | solution.py:288
  12.8 4.6 %collective-permute-start.1 = (f32[40,256]{1,0:T(8,128)}, f32[40,256]{1,0:T(8,128)S(1)}, u32[]{:S(2)}, u32[]{:S(2)}) collective-permute-start(f32[40,256]{1,0:T(8,128)} %get-tuple-element.24), channel_id=1, source_target_pairs={{0,8},{8,16},{16,24},{24,32},{32,40},{40,48},{48,56},{1,9},{9,17},... | collective-permute-start | bytes 122888 | tf_op jit(solution)/shard_map/ppermute | solution.py:392
  17.5 1.4 %collective-permute-done.1.yin_ref = f32[40,256]{1,0:T(8,128)S(1)} collective-permute-done((f32[40,256]{1,0:T(8,128)}, f32[40,256]{1,0:T(8,128)S(1)}, u32[]{:S(2)}, u32[]{:S(2)}) %collective-permute-start.1) | collective-permute-done | bytes 40992 | tf_op jit(solution)/shard_map/ppermute | solution.py:392
  18.9 0.0 copy-start.1
  18.9 0.8 %select_add_fusion = f32[32,128]{1,0:T(8,128)S(1)} fusion(f32[40,128]{1,0:T(8,128)} %get-tuple-element.25, f32[128]{0:T(128)S(1)} %slice_bitcast_fusion, pred[32]{0:T(512)(128)(4,1)S(1)} %iota_compare_fusion), kind=kLoop, calls=%fused_computation | loop fusion | flops 8192 | bytes 33312 | tf_op jit(solution)/shard_map/add | solution.py:402
  19.7 3.5 %collective-permute-start.2 = (f32[32,128]{1,0:T(8,128)S(1)}, f32[32,128]{1,0:T(8,128)S(1)}, u32[]{:S(2)}, u32[]{:S(2)}) collective-permute-start(f32[32,128]{1,0:T(8,128)S(1)} %select_add_fusion), channel_id=1, source_target_pairs={{0,1},{1,2},{2,3},{3,4},{4,5},{5,6},{6,7},{8,9},{9,10},{10,11},{11... | collective-permute-start | bytes 49160 | tf_op jit(solution)/shard_map/ppermute | solution.py:392
  23.2 0.9 %collective-permute-done.2.zin_ref = f32[32,128]{1,0:T(8,128)S(1)} collective-permute-done((f32[32,128]{1,0:T(8,128)S(1)}, f32[32,128]{1,0:T(8,128)S(1)}, u32[]{:S(2)}, u32[]{:S(2)}) %collective-permute-start.2) | collective-permute-done | bytes 16416 | tf_op jit(solution)/shard_map/ppermute | solution.py:392
  24.1 0.0 copy-start.2
  24.1 0.0 copy-done.1
  24.1 0.6 copy-done.2
  24.7 2.4 %finish.1 = (f32[32,32,128]{2,1,0:T(8,128)}, f32[16,16,128]{2,1,0:T(8,128)}, f32[8,8,128]{2,1,0:T(8,128)}, f32[4,8,128]{2,1,0:T(8,128)}, f32[2,8,128]{2,1,0:T(8,128)}, /*index=5*/f32[256,128]{1,0:T(8,128)}) custom-call(f32[1320,128]{1,0:T(8,128)} %get-tuple-element.19.first_ref, f32[616,128]{1,0:T(8,128)} %get-tuple-element.20.rest_ref, f32[40,256]{1,0:T(8,128)} %copy-done, ...), custom_call_target="tpu_custom_call" | custom-call | tf_op jit(solution)/shard_map/finish/pallas_call | solution.py:341
  27.0 31.7 %all_to_all.11 = f32[256,1,128]{2,1,0:T(1,128)} all-to-all(f32[256,1,128]{2,1,0:T(1,128)} %bitcast.7), channel_id=1, replica_groups=mesh['gx'=4,'gy_0'=4,'gy_1'=2,'gz'=8] {'gx','gy_0','gy_1','gz'}, dimensions={0} | all-to-all | bytes 262144 | tf_op jit(solution)/shard_map/all_to_all | solution.py:404
  58.7 2.1 %scale.1 = (f32[32,32,128]{2,1,0:T(8,128)}, f32[16,16,64]{2,1,0:T(8,128)}, f32[8,8,32]{2,1,0:T(8,128)}, f32[4,4,16]{2,1,0:T(4,128)}, f32[2,2,8]{2,1,0:T(2,128)}, /*index=5*/f32[5]{0:T(128)}) custom-call(f32[256,128]{1,0:T(8,128)} %bitcast.6, f32[32,32,128]{2,1,0:T(8,128)} %get-tuple-element.27.refs_0_, f32[16,16,128]{2,1,0:T(8,128)} %get-tuple-element.28.refs_1_, ...), custom_call_target="tpu_custom_call" | custom-call | tf_op jit(solution)/shard_map/scale/pallas_call | solution.py:382
  (2 shorter events, 0.0 us)
Async XLA Ops:
  5.4 5.3 %collective-permute-start = (f32[40,256]{1,0:T(8,128)}, f32[40,256]{1,0:T(8,128)S(1)}, u32[]{:S(2)}, u32[]{:S(2)}) collective-permute-start(f32[40,256]{1,0:T(8,128)} %get-tuple-element.21), channel_id=1, source_target_pairs={{0,64},{64,128},{128,192},{1,65},{65,129},{129,193},{2,66},{66,130... | collective-permute-start | bytes 122888 | tf_op jit(solution)/shard_map/ppermute | solution.py:392
  10.8 0.6 %copy-start = (f32[40,256]{1,0:T(8,128)}, f32[40,256]{1,0:T(8,128)S(1)}, u32[]{:S(2)}) copy-start(f32[40,256]{1,0:T(8,128)S(1)} %collective-permute-done.xin_ref) | copy-start | bytes 122884
  12.8 6.0 %collective-permute-start.1 = (f32[40,256]{1,0:T(8,128)}, f32[40,256]{1,0:T(8,128)S(1)}, u32[]{:S(2)}, u32[]{:S(2)}) collective-permute-start(f32[40,256]{1,0:T(8,128)} %get-tuple-element.24), channel_id=1, source_target_pairs={{0,8},{8,16},{16,24},{24,32},{32,40},{40,48},{48,56},{1,9},{9,17},... | collective-permute-start | bytes 122888 | tf_op jit(solution)/shard_map/ppermute | solution.py:392
  18.9 5.2 %copy-start.1 = (f32[40,256]{1,0:T(8,128)}, f32[40,256]{1,0:T(8,128)S(1)}, u32[]{:S(2)}) copy-start(f32[40,256]{1,0:T(8,128)S(1)} %collective-permute-done.1.yin_ref) | copy-start | bytes 122884
  19.7 4.4 %collective-permute-start.2 = (f32[32,128]{1,0:T(8,128)S(1)}, f32[32,128]{1,0:T(8,128)S(1)}, u32[]{:S(2)}, u32[]{:S(2)}) collective-permute-start(f32[32,128]{1,0:T(8,128)S(1)} %select_add_fusion), channel_id=1, source_target_pairs={{0,1},{1,2},{2,3},{3,4},{4,5},{5,6},{6,7},{8,9},{9,10},{10,11},{11... | collective-permute-start | bytes 49160 | tf_op jit(solution)/shard_map/ppermute | solution.py:392
  24.1 0.6 copy-start.2

commit v2 on v1

--- a/solution.py
+++ b/solution.py
@@ -1,3 +1,5 @@
+import math
+
 import jax
 import jax.numpy as jnp
 from jax import lax
@@ -7,7 +9,9 @@
 from jax.sharding import PartitionSpec as P
 
 LEVELS = 5
+GX = ("gx",)
 GY = ("gy_0", "gy_1")
+GZ = ("gz",)
 GX_GY_GZ = ("gx", "gy_0", "gy_1", "gz")
 EPSILON = 1e-06
 
@@ -189,6 +193,7 @@
         at = (0 if level == 0 else REST_AT[level]) + plane * ROWS[level]
         return ref[pl.ds(at, ROWS[level]), :]
 
+    keep_x = sends(GX)
     xface_ref[:, :LANES] = first_ref[pl.ds(last, ROWS[0]), :]
     tile = jnp.where(iota((ROWS[0], LANES), 1) == END_AT, right_rows(0, COUNT[0]), 0.0)
     xface_ref[:, LANES:] = tile
@@ -197,6 +202,7 @@
         keep = tile_mask(level, shape) | (iota(shape, 1) == END_AT + level)
         old = xface_ref[pl.ds(0, ROWS[level]), LANES:]
         xface_ref[pl.ds(0, ROWS[level]), LANES:] = jnp.where(keep, right_rows(level, COUNT[level]), old)
+    xface_ref[...] = xface_ref[...] * keep_x
 
     yface_ref[:, :LANES] = first_ref[pl.ds(COUNT[0], COUNT[0], stride=ROWS[0]), :]
     yface_ref[:, LANES:] = jnp.zeros((COUNT[0], LANES), jnp.float32)
@@ -248,11 +254,11 @@
     return pl.pallas_call(
         local_kernel,
         out_shape=(
-            jax.ShapeDtypeStruct((FIRST_ROWS, LANES), f32),
-            jax.ShapeDtypeStruct((REST_ROWS, LANES), f32),
-            jax.ShapeDtypeStruct((ROWS[0], BZ), f32),
-            jax.ShapeDtypeStruct((COUNT[0], BZ), f32),
-            jax.ShapeDtypeStruct((ROWS[0], LANES), f32),
+            pltpu.VMEM((FIRST_ROWS, LANES), f32),
+            pltpu.VMEM((REST_ROWS, LANES), f32),
+            pltpu.VMEM((ROWS[0], BZ), f32),
+            pltpu.VMEM((COUNT[0], BZ), f32),
+            pltpu.VMEM((ROWS[0], LANES), f32),
         ),
         in_specs=[pl.BlockSpec(memory_space=pl.ANY)],
         out_specs=(vmem,) * 5,
@@ -261,25 +267,37 @@
     )(block)
 
 
-def edge_kernel(xin_ref, yface_ref, zface_ref, yout_ref, zout_ref):
+def edge_kernel(xin_ref, yface_ref, zface_ref, yout_ref, zout_ref, yzout_ref):
     count = COUNT[0]
     lane = iota((ROWS[0], LANES), 1)
     zface = zface_ref[...] + jnp.where(lane >= END_AT, xin_ref[:, LANES:], 0.0)
-    zout_ref[...] = zface
+    keep_y = sends(GY)
+    keep_z = sends(GZ)
+    zout_ref[...] = zface[:count] * keep_z
     row = iota((count, LANES), 0)
-    yout_ref[pl.ds(0, count), :LANES] = yface_ref[:, :LANES] + jnp.where(
-        row == 0, xin_ref[pl.ds(count, 1), :LANES], 0.0
-    )
+    yout_ref[:, :LANES] = (
+        yface_ref[:, :LANES] + jnp.where(row == 0, xin_ref[pl.ds(count, 1), :LANES], 0.0)
+    ) * keep_y
     edge = jnp.zeros((1, LANES), jnp.float32)
     corner = jnp.zeros((1, LANES), jnp.float32)
     for level in range(LEVELS):
-        at = pl.ds(COUNT[level], 1)
+        at = COUNT[level]
         if level:
-            edge = jnp.where(tile_mask(level, (1, LANES)), xin_ref[at, LANES:], edge)
-        corner = jnp.where(face_mask(level, (1, LANES)), zout_ref[at, :], corner)
-    yout_ref[pl.ds(0, count), LANES:] = yface_ref[:, LANES:] + jnp.where(row == 0, edge, 0.0)
-    yout_ref[pl.ds(count, 8), :LANES] = jnp.where(iota((8, LANES), 0) == 0, corner, 0.0)
-    yout_ref[pl.ds(count, 8), LANES:] = jnp.zeros((8, LANES), jnp.float32)
+            edge = jnp.where(tile_mask(level, (1, LANES)), xin_ref[pl.ds(at, 1), LANES:], edge)
+        corner = jnp.where(face_mask(level, (1, LANES)), zface[at : at + 1], corner)
+    yout_ref[:, LANES:] = (yface_ref[:, LANES:] + jnp.where(row == 0, edge, 0.0)) * keep_y
+    yzout_ref[...] = jnp.where(iota((8, LANES), 0) == 0, corner, 0.0) * (keep_y * keep_z)
+
+
+def sends(axis):
+    index = 0
+    for name in axis:
+        index = index * lax.axis_size(name) + lax.axis_index(name)
+    return jnp.where(index < lax.axis_size(axis) - 1, 1.0, 0.0)
+
+
+def resident(*arrays):
+    return [pltpu.with_memory_space_constraint(array, pltpu.VMEM) for array in arrays]
 
 
 def add_edges(xin, yface, zface):
@@ -288,17 +306,20 @@
     return pl.pallas_call(
         edge_kernel,
         out_shape=(
-            jax.ShapeDtypeStruct((ROWS[0], BZ), f32),
-            jax.ShapeDtypeStruct((ROWS[0], LANES), f32),
+            pltpu.VMEM((COUNT[0], BZ), f32),
+            pltpu.VMEM((COUNT[0], LANES), f32),
+            pltpu.VMEM((8, LANES), f32),
         ),
         in_specs=[vmem] * 3,
-        out_specs=(vmem,) * 2,
+        out_specs=(vmem,) * 3,
         name="edges",
-    )(xin, yface, zface)
-
-
-def finish_kernel(first_ref, rest_ref, xin_ref, yin_ref, zin_ref, *out_refs):
+    )(*resident(xin, yface, zface))
+
+
+def finish_kernel(first_ref, rest_ref, xin_ref, yin_ref, zin_ref, yzin_ref, *out_refs):
     sums_ref = out_refs[LEVELS]
+    corner = yzin_ref[...]
+    zface = jnp.concatenate([zin_ref[pl.ds(0, 8), :] + corner, zin_ref[pl.ds(8, COUNT[0] - 8), :]], axis=0)
     sums = jnp.zeros((1, LANES), jnp.float32)
     for level in range(LEVELS):
         count = COUNT[level]
@@ -318,7 +339,7 @@
             if rows > 8:
                 yrow = jnp.concatenate([yrow, jnp.zeros((rows - 8, LANES), jnp.float32)], axis=0)
             shift = (LANE_AT[level] - face_lane(level, plane)) % LANES
-            zcol = zin_ref[pl.ds(0, rows), :]
+            zcol = zface[:rows]
             if shift:
                 zcol = pltpu.roll(zcol, shift, 1)
             values = values + yrow + jnp.where(zlane, zcol, 0.0)
@@ -333,18 +354,18 @@
     sums_ref[...] = jnp.broadcast_to(sums, sums_ref.shape)
 
 
-def finish_levels(first, rest, xin, yin, zin, devices):
+def finish_levels(first, rest, xin, yin, zin, yzin, devices):
     f32 = jnp.float32
     vmem = pl.BlockSpec(memory_space=pltpu.VMEM)
     shapes = [(COUNT[level], max(COUNT[level], 8), LANES) for level in range(LEVELS)]
     shapes.append((devices, LANES))
     return pl.pallas_call(
         finish_kernel,
-        out_shape=tuple(jax.ShapeDtypeStruct(shape, f32) for shape in shapes),
-        in_specs=[vmem] * 5,
+        out_shape=tuple(pltpu.VMEM(shape, f32) for shape in shapes),
+        in_specs=[vmem] * 6,
         out_specs=(vmem,) * 6,
         name="finish",
-    )(first, rest, xin, yin, zin)
+    )(*resident(first, rest, xin, yin, zin, yzin))
 
 
 def scale_kernel(sums_ref, *refs):
@@ -385,22 +406,29 @@
         in_specs=[vmem] * 6,
         out_specs=(vmem,) * 6,
         name="scale",
-    )(sums, *levels)
-
-
-def to_next(face, axis):
-    return lax.ppermute(face, axis, [(i, i + 1) for i in range(lax.axis_size(axis) - 1)])
+    )(*resident(sums, *levels))
+
+
+def to_next(face, *axes):
+    sizes = [lax.axis_size(axis) for axis in axes]
+    route = []
+    for source in range(math.prod(sizes)):
+        target, rest, scale = 0, source, 1
+        for size in reversed(sizes):
+            target += (rest % size + 1) % size * scale
+            rest //= size
+            scale *= size
+        route.append((source, target))
+    return lax.ppermute(face, sum(axes, ()), route)
 
 
 def per_device(residual_in):
     devices = lax.axis_size(GX_GY_GZ)
     first, rest, xface, yface, zface = local_restriction(residual_in)
-    xin = to_next(xface, "gx")
-    yface, zface = add_edges(xin, yface, zface)
-    yin = to_next(yface, GY)
-    corner = jnp.where(iota((COUNT[0], LANES), 0) == 0, yin[COUNT[0], :LANES], 0.0)
-    zin = to_next(zface[: COUNT[0]] + corner, "gz")
-    *levels, sums = finish_levels(first, rest, xin, yin, zin, devices)
+    xin = to_next(xface, GX)
+    yface, zface, edge = add_edges(xin, yface, zface)
+    yin, zin, edgein = to_next(yface, GY), to_next(zface, GZ), to_next(edge, GY, GZ)
+    *levels, sums = finish_levels(first, rest, xin, yin, zin, edgein, devices)
     sums = lax.all_to_all(sums, GX_GY_GZ, 0, 0, tiled=True)
     return tuple(scale_levels(sums, levels))
 

time: 61.2 us -> 45 us (0.74)
  blocking collectives: 31.7 us -> 24.2 us
  Pallas kernels: 10.7 us -> 5.39 us
  starting transfers between devices: 12.1 us -> 8.68 us
  waiting for transfers between devices: 3.63 us -> 6 us
  local copies, waits for them, and re-layouts: 1.22 us -> 0 us
  other arithmetic: 0.81 us -> 0 us
    all_to_all x1, blocking collectives: 31.7 us -> 24.2 us  [per_device(): sums = lax.all_to_all(sums, GX_GY_GZ, 0, 0, tiled=True)]
    pallas_call x3, Pallas kernels: 8.61 us -> 4.37 us  [the longest x1 4.01 us: local_restriction(): pl.pallas_call(local_kernel, out_shape=(pltpu.VMEM((FIRST_ROWS, LANES), f...]
    ppermute x3 -> x4, starting transfers between devices: 12.1 us -> 8.68 us  [to_next(): return lax.ppermute(face, sum(axes, ()), route)]
    ppermute x3 -> x4, waiting for transfers between devices: 3.63 us -> 6 us  [to_next(): return lax.ppermute(face, sum(axes, ()), route)]
    unnamed x6 -> x0, local copies, waits for them, and re-layouts: 1.22 us -> none
    pallas_call x1, Pallas kernels: 2.13 us -> 1.01 us  [scale_levels(): pl.pallas_call(scale_kernel, out_shape=tuple((jax.ShapeDtypeStruct(shape,...]
    add x1 -> x0, other arithmetic: 0.8 us -> none  [per_device(): zin = to_next(zface[:COUNT[0]] + corner, 'gz')]
  transfers between devices with their start and end apart: 3 -> 4, of which waited for: 3 -> 3; matrix products, arithmetic and copies ran while one was open for 0% -> 0% of each run, Pallas kernels for 0% -> 0%
where the time goes in v2:
time: 45 us; the launch traced here: 44.9 us
  blocking collectives  24.2 us (54%)
  starting transfers between devices  8.68 us (19%)
  waiting for transfers between devices  6 us (13%)
  Pallas kernels  5.39 us (12%)
  between operations  0.66 us (1%)
    all_to_all x1, blocking collectives, per_device(): sums = lax.all_to_all(sums, GX_GY_GZ, 0, 0, tiled=True)  24.2 us
    ppermute x4, starting transfers between devices, to_next(): return lax.ppermute(face, sum(axes, ()), route)  8.68 us
    ppermute x4, waiting for transfers between devices, to_next(): return lax.ppermute(face, sum(axes, ()), route)  6 us
    pallas_call x1, Pallas kernels, local_restriction(): pl.pallas_call(local_kernel, out_shape=(pltpu.VMEM((FIRST_ROWS, LANES), f...  4.01 us
    pallas_call x1, Pallas kernels, scale_levels(): pl.pallas_call(scale_kernel, out_shape=tuple((jax.ShapeDtypeStruct(shape,...  1.01 us
  transfers between devices with their start and end apart: 4, of which 3 were waited for; matrix products, arithmetic and copies ran while one was open for 0% of the time, Pallas kernels for 0%

profile of v2, /device:TPU:1, one launch (start us, length us, event | category | flops | bytes accessed | tf_op | source)
XLA Modules:
  0.0 44.9 jit_solution(9358791294446778819)
XLA Ops:
  0.6 4.0 %local_levels.1 = (f32[1320,128]{1,0:T(8,128)S(1)}, f32[616,128]{1,0:T(8,128)S(1)}, f32[40,256]{1,0:T(8,128)S(1)}, f32[32,256]{1,0:T(8,128)S(1)}, f32[40,128]{1,0:T(8,128)S(1)}) custom-call(f32[64,64,256]{2,1,0:T(8,128)} %grid_ref.1), custom_call_target="tpu_custom_call" | custom-call | tf_op jit(solution)/shard_map/local_levels/pallas_call | solution.py:254
  4.7 2.1 %collective-permute-start = (f32[40,256]{1,0:T(8,128)S(1)}, f32[40,256]{1,0:T(8,128)S(1)}, u32[]{:S(2)}, u32[]{:S(2)}) collective-permute-start(f32[40,256]{1,0:T(8,128)S(1)} %get-tuple-element.22), channel_id=1, source_target_pairs={{0,64},{64,128},{128,192},{192,0},{1,65},{65,129},{129,193},{193,1... | collective-permute-start | bytes 122888 | tf_op jit(solution)/shard_map/ppermute | solution.py:422
  6.8 2.7 %collective-permute-done.xin_ref = f32[40,256]{1,0:T(8,128)S(1)} collective-permute-done((f32[40,256]{1,0:T(8,128)S(1)}, f32[40,256]{1,0:T(8,128)S(1)}, u32[]{:S(2)}, u32[]{:S(2)}) %collective-permute-start) | collective-permute-done | bytes 40992 | tf_op jit(solution)/shard_map/ppermute | solution.py:422
  9.4 3.2 %collective-permute-start.1 = (f32[32,256]{1,0:T(8,128)S(1)}, f32[32,256]{1,0:T(8,128)S(1)}, u32[]{:S(2)}, u32[]{:S(2)}) collective-permute-start(f32[32,256]{1,0:T(8,128)S(1)} %get-tuple-element.25), channel_id=1, source_target_pairs={{0,8},{8,16},{16,24},{24,32},{32,40},{40,48},{48,56},{56,0},{1,9},... | collective-permute-start | bytes 98312 | tf_op jit(solution)/shard_map/ppermute | solution.py:422
  12.7 1.6 %collective-permute-start.2 = (f32[32,128]{1,0:T(8,128)S(1)}, f32[32,128]{1,0:T(8,128)S(1)}, u32[]{:S(2)}, u32[]{:S(2)}) collective-permute-start(f32[32,128]{1,0:T(8,128)S(1)} %get-tuple-element.26), channel_id=1, source_target_pairs={{0,1},{1,2},{2,3},{3,4},{4,5},{5,6},{6,7},{7,0},{8,9},{9,10},{10,1... | collective-permute-start | bytes 49160 | tf_op jit(solution)/shard_map/ppermute | solution.py:422
  14.3 1.7 %collective-permute-start.3 = (f32[8,128]{1,0:T(8,128)S(1)}, f32[8,128]{1,0:T(8,128)S(1)}, u32[]{:S(2)}, u32[]{:S(2)}) collective-permute-start(f32[8,128]{1,0:T(8,128)S(1)} %get-tuple-element.27), channel_id=1, source_target_pairs={{0,9},{1,10},{2,11},{3,12},{4,13},{5,14},{6,15},{7,8},{8,17},{9,18... | collective-permute-start | bytes 12296 | tf_op jit(solution)/shard_map/ppermute | solution.py:422
  16.0 2.7 %collective-permute-done.3.yzin_ref = f32[8,128]{1,0:T(8,128)S(1)} collective-permute-done((f32[8,128]{1,0:T(8,128)S(1)}, f32[8,128]{1,0:T(8,128)S(1)}, u32[]{:S(2)}, u32[]{:S(2)}) %collective-permute-start.3) | collective-permute-done | bytes 4128 | tf_op jit(solution)/shard_map/ppermute | solution.py:422
  18.7 0.6 %collective-permute-done.2.zin_ref = f32[32,128]{1,0:T(8,128)S(1)} collective-permute-done((f32[32,128]{1,0:T(8,128)S(1)}, f32[32,128]{1,0:T(8,128)S(1)}, u32[]{:S(2)}, u32[]{:S(2)}) %collective-permute-start.2) | collective-permute-done | bytes 16416 | tf_op jit(solution)/shard_map/ppermute | solution.py:422
  19.4 0.0 collective-permute-done.1.yin_ref
  19.4 0.3 finish.1
  19.7 24.2 %all_to_all.11 = f32[256,1,128]{2,1,0:T(1,128)S(1)} all-to-all(f32[256,1,128]{2,1,0:T(1,128)S(1)} %bitcast.5), channel_id=1, replica_groups=mesh['gx'=4,'gy_0'=4,'gy_1'=2,'gz'=8] {'gx','gy_0','gy_1','gz'}, dimensions={0} | all-to-all | bytes 262144 | tf_op jit(solution)/shard_map/all_to_all | solution.py:432
  43.9 1.0 %scale.1 = (f32[32,32,128]{2,1,0:T(8,128)}, f32[16,16,64]{2,1,0:T(8,128)}, f32[8,8,32]{2,1,0:T(8,128)}, f32[4,4,16]{2,1,0:T(4,128)}, f32[2,2,8]{2,1,0:T(2,128)}, /*index=5*/f32[5]{0:T(128)}) custom-call(f32[256,128]{1,0:T(8,128)S(1)} %bitcast.4, f32[32,32,128]{2,1,0:T(8,128)S(1)} %get-tuple-element.29.refs_0_, f32[16,16,128]{2,1,0:T(8,128)S(1)} %get-tuple-element.30.refs_1_, ...), custom_call_target="tpu_custom_call" | custom-call | tf_op jit(solution)/shard_map/scale/pallas_call | solution.py:403
  (1 shorter events, 0.0 us)
Async XLA Ops:
  4.7 4.8 %collective-permute-start = (f32[40,256]{1,0:T(8,128)S(1)}, f32[40,256]{1,0:T(8,128)S(1)}, u32[]{:S(2)}, u32[]{:S(2)}) collective-permute-start(f32[40,256]{1,0:T(8,128)S(1)} %get-tuple-element.22), channel_id=1, source_target_pairs={{0,64},{64,128},{128,192},{192,0},{1,65},{65,129},{129,193},{193,1... | collective-permute-start | bytes 122888 | tf_op jit(solution)/shard_map/ppermute | solution.py:422
  9.4 9.9 %collective-permute-start.1 = (f32[32,256]{1,0:T(8,128)S(1)}, f32[32,256]{1,0:T(8,128)S(1)}, u32[]{:S(2)}, u32[]{:S(2)}) collective-permute-start(f32[32,256]{1,0:T(8,128)S(1)} %get-tuple-element.25), channel_id=1, source_target_pairs={{0,8},{8,16},{16,24},{24,32},{32,40},{40,48},{48,56},{56,0},{1,9},... | collective-permute-start | bytes 98312 | tf_op jit(solution)/shard_map/ppermute | solution.py:422
  12.7 6.7 %collective-permute-start.2 = (f32[32,128]{1,0:T(8,128)S(1)}, f32[32,128]{1,0:T(8,128)S(1)}, u32[]{:S(2)}, u32[]{:S(2)}) collective-permute-start(f32[32,128]{1,0:T(8,128)S(1)} %get-tuple-element.26), channel_id=1, source_target_pairs={{0,1},{1,2},{2,3},{3,4},{4,5},{5,6},{6,7},{7,0},{8,9},{9,10},{10,1... | collective-permute-start | bytes 49160 | tf_op jit(solution)/shard_map/ppermute | solution.py:422
  14.3 4.5 %collective-permute-start.3 = (f32[8,128]{1,0:T(8,128)S(1)}, f32[8,128]{1,0:T(8,128)S(1)}, u32[]{:S(2)}, u32[]{:S(2)}) collective-permute-start(f32[8,128]{1,0:T(8,128)S(1)} %get-tuple-element.27), channel_id=1, source_target_pairs={{0,9},{1,10},{2,11},{3,12},{4,13},{5,14},{6,15},{7,8},{8,17},{9,18... | collective-permute-start | bytes 12296 | tf_op jit(solution)/shard_map/ppermute | solution.py:422

commit v3 on v2

--- a/solution.py
+++ b/solution.py
@@ -24,6 +24,8 @@
 REST_AT = [0, 0, 408, 552, 592]
 REST_ROWS = 616
 FIRST_ROWS = (COUNT[0] + 1) * ROWS[0]
+HIGH_PLANES = [17, 8, 4, 2, 1]
+LOW_PLANES = [17, 9, 5, 3, 2]
 LANE_AT = [0, 0, 64, 96, 112]
 LANE_COUNT = [128, 64, 32, 16, 8]
 END_AT = 120
@@ -98,111 +100,206 @@
     return parts[0] if len(parts) == 1 else jnp.concatenate(parts, axis=0)
 
 
-def local_kernel(grid_ref, first_ref, rest_ref, xface_ref, yface_ref, zface_ref, *scratch):
-    block_ref, plane_ref, stack_ref, end_ref, sems = scratch[:5]
-    pass_refs = [scratch[5 + 2 * level : 7 + 2 * level] for level in range(LEVELS)]
+def high_from(level):
+    return COUNT[level] // 2 + 1
+
+
+def pass_scratch(planes):
+    shapes = [(count * PASS_ROWS[level], LANES) for level, count in enumerate(planes)]
+    return [pltpu.VMEM(shape, jnp.float32) for shape in shapes for _ in range(2)]
+
+
+def clear_rims(pass_refs, planes):
+    for level in range(LEVELS):
+        body = BY if level == 0 else ROWS[level - 1]
+        tail = PASS_ROWS[level] - 8 - body
+        for ref in pass_refs[2 * level : 2 * level + 2]:
+            for plane in range(planes[level]):
+                base = plane * PASS_ROWS[level]
+                ref[pl.ds(base, 8), :] = jnp.zeros((8, LANES), jnp.float32)
+                if tail:
+                    ref[pl.ds(base + 8 + body, tail), :] = jnp.zeros((tail, LANES), jnp.float32)
+
+
+def first_planes(block_ref, pass_refs, plane_ref, planes, offset):
+    for plane in planes:
+        for half in range(2):
+            lanes = slice(half * LANES, (half + 1) * LANES)
+            before = block_ref[2 * plane, :, lanes]
+            middle = block_ref[2 * plane + 1, :, lanes]
+            after = block_ref[2 * plane + 2, :, lanes]
+            pass_refs[half][pl.ds(aligned(plane * PASS_ROWS[0]) + 8, BY), :] = (
+                before + after + (middle + middle)
+            )
+    for plane in planes:
+        first_y(pass_refs, plane_ref, plane, offset)
+
+
+def first_y(pass_refs, plane_ref, plane, offset):
+    for half in range(2):
+        lanes = slice(half * LANES, (half + 1) * LANES)
+        at = aligned((plane + offset) * ROWS[0])
+        plane_ref[pl.ds(at, ROWS[0]), lanes] = y_pass(pass_refs[half], plane, 0)
+
+
+def later_planes(level, planes, load, pass_refs, stack_ref):
+    for half in range(2):
+        lanes = slice(half * LANES, (half + 1) * LANES)
+        ref = pass_refs[2 * level + half]
+        for local, plane in enumerate(planes):
+            middle = load(2 * plane, lanes)
+            total = middle + middle
+            if plane > 0:
+                total += load(2 * plane - 1, lanes)
+            if plane < COUNT[level]:
+                total += load(2 * plane + 1, lanes)
+            ref[pl.ds(local * PASS_ROWS[level] + 8, ROWS[level - 1]), :] = total
+        for local, plane in enumerate(planes):
+            at = REST_AT[level] + plane * ROWS[level]
+            stack_ref[pl.ds(at, ROWS[level]), lanes] = y_pass(ref, local, level)
+
+
+def high_kernel(grid_ref, plane_ref, stack_ref, xface_ref, block_ref, sems, *pass_refs):
+    half_x = BX // 2
+    chunks = half_x // CHUNK
 
     def chunk_copy(index):
         return pltpu.make_async_copy(
-            grid_ref.at[pl.ds(index * CHUNK, CHUNK)],
+            grid_ref.at[pl.ds(half_x + index * CHUNK, CHUNK)],
             block_ref.at[pl.ds(index * CHUNK + 1, CHUNK)],
             sems.at[index],
         )
 
-    chunks = BX // CHUNK
     for index in range(chunks):
         chunk_copy(index).start()
     table = stencil_table()
     block_ref[0] = jnp.zeros((BY, BZ), jnp.float32)
-    for level in range(LEVELS):
-        body = BY if level == 0 else ROWS[level - 1]
-        tail = PASS_ROWS[level] - 8 - body
-        for half in range(2):
-            ref = pass_refs[level][half]
-            for plane in range(COUNT[level] + 1):
-                base = plane * PASS_ROWS[level]
-                ref[pl.ds(base, 8), :] = jnp.zeros((8, LANES), jnp.float32)
-                if tail:
-                    ref[pl.ds(base + 8 + body, tail), :] = jnp.zeros((tail, LANES), jnp.float32)
-
-    def first_y(plane):
-        for half in range(2):
-            lanes = slice(half * LANES, (half + 1) * LANES)
-            out = y_pass(pass_refs[0][half], plane, 0)
-            plane_ref[pl.ds(aligned(plane * ROWS[0]), ROWS[0]), lanes] = out
-
-    def first_level(index, carry):
+    clear_rims(pass_refs, HIGH_PLANES)
+
+    def step(index, carry):
         chunk_copy(index).wait()
-        for part in range(CHUNK // 2):
-            plane = index * (CHUNK // 2) + part
-            for half in range(2):
-                lanes = slice(half * LANES, (half + 1) * LANES)
-                before = block_ref[2 * plane, :, lanes]
-                middle = block_ref[2 * plane + 1, :, lanes]
-                after = block_ref[2 * plane + 2, :, lanes]
-                pass_refs[0][half][pl.ds(aligned(plane * PASS_ROWS[0]) + 8, BY), :] = (
-                    before + after + (middle + middle)
-                )
-        for part in range(CHUNK // 2):
-            first_y(index * (CHUNK // 2) + part)
+        planes = [index * (CHUNK // 2) + part for part in range(CHUNK // 2)]
+        first_planes(block_ref, pass_refs, plane_ref, planes, COUNT[0] // 2)
         return carry
 
-    lax.fori_loop(0, chunks, first_level, 0)
+    lax.fori_loop(0, chunks, step, 0)
     for half in range(2):
         lanes = slice(half * LANES, (half + 1) * LANES)
-        pass_refs[0][half][pl.ds(COUNT[0] * PASS_ROWS[0] + 8, BY), :] = block_ref[BX, :, lanes]
-    first_y(COUNT[0])
-
+        at = COUNT[0] // 2 * PASS_ROWS[0] + 8
+        pass_refs[half][pl.ds(at, BY), :] = block_ref[half_x, :, lanes]
+    first_y(pass_refs, plane_ref, COUNT[0] // 2, COUNT[0] // 2)
     for level in range(1, LEVELS):
-        source = plane_ref if level == 1 else stack_ref
-        source_at = REST_AT[level - 1] if level > 1 else 0
-        rows = ROWS[level - 1]
-        for half in range(2):
-            lanes = slice(half * LANES, (half + 1) * LANES)
-            ref = pass_refs[level][half]
-            for plane in range(COUNT[level] + 1):
-                middle = source[pl.ds(source_at + 2 * plane * rows, rows), lanes]
-                total = middle + middle
-                if plane > 0:
-                    total += source[pl.ds(source_at + (2 * plane - 1) * rows, rows), lanes]
-                if plane < COUNT[level]:
-                    total += source[pl.ds(source_at + (2 * plane + 1) * rows, rows), lanes]
-                ref[pl.ds(plane * PASS_ROWS[level] + 8, rows), :] = total
-            for plane in range(COUNT[level] + 1):
-                at = REST_AT[level] + plane * ROWS[level]
-                stack_ref[pl.ds(at, ROWS[level]), lanes] = y_pass(ref, plane, level)
-
-    span = 8 * ROWS[0]
-
-    def first_z(index, carry):
-        at = aligned(index * span)
-        both = apply_table(plane_ref[pl.ds(at, span), :], table)
-        first_ref[pl.ds(at, span), :] = both[:, :LANES]
-        end_ref[pl.ds(at, span), :] = both[:, LANES:]
+
+        def load(plane, lanes, level=level):
+            source = plane_ref if level == 1 else stack_ref
+            at = (REST_AT[level - 1] if level > 1 else 0) + plane * ROWS[level - 1]
+            return source[pl.ds(at, ROWS[level - 1]), lanes]
+
+        later_planes(level, range(high_from(level), COUNT[level] + 1), load, pass_refs, stack_ref)
+
+    keep_x = sends(GX)
+    parts = [plane_ref[pl.ds(COUNT[0] * ROWS[0], ROWS[0]), :]]
+    for level in range(1, LEVELS):
+        parts.append(stack_ref[pl.ds(REST_AT[level] + COUNT[level] * ROWS[level], ROWS[level]), :])
+    faces = apply_table(jnp.concatenate(parts, axis=0), table) * keep_x
+    xface_ref[:, :LANES] = faces[: ROWS[0], :LANES]
+    tiles = [jnp.where(iota((ROWS[0], LANES), 1) == END_AT, faces[: ROWS[0], LANES:], 0.0)]
+    at = ROWS[0]
+    for level in range(1, LEVELS):
+        shape = (ROWS[level], LANES)
+        keep = tile_mask(level, shape) | (iota(shape, 1) == END_AT + level)
+        face = jnp.where(keep, faces[at : at + ROWS[level], LANES:], 0.0)
+        at += ROWS[level]
+        if ROWS[level] < ROWS[0]:
+            blank = jnp.zeros((ROWS[0] - ROWS[level], LANES), jnp.float32)
+            face = jnp.concatenate([face, blank], axis=0)
+        tiles.append(face)
+    xface_ref[:, LANES:] = sum(tiles[1:], tiles[0])
+
+
+def high_half(block):
+    f32 = jnp.float32
+    vmem = pl.BlockSpec(memory_space=pltpu.VMEM)
+    return pl.pallas_call(
+        high_kernel,
+        out_shape=(
+            pltpu.VMEM((FIRST_ROWS, BZ), f32),
+            pltpu.VMEM((REST_ROWS, BZ), f32),
+            pltpu.VMEM((ROWS[0], BZ), f32),
+        ),
+        in_specs=[pl.BlockSpec(memory_space=pl.ANY)],
+        out_specs=(vmem,) * 3,
+        scratch_shapes=[
+            pltpu.VMEM((BX // 2 + 1, BY, BZ), f32),
+            pltpu.SemaphoreType.DMA((BX // 2 // CHUNK,)),
+        ]
+        + pass_scratch(HIGH_PLANES),
+        name="high_half",
+    )(block)
+
+
+def low_kernel(grid_ref, high_ref, highs_ref, first_ref, rest_ref, yface_ref, zface_ref, *scratch):
+    block_ref, plane_ref, stack_ref, end_ref, sems = scratch[:5]
+    pass_refs = scratch[5:]
+    half_x = BX // 2
+    chunks = half_x // CHUNK
+    low = high_from(0)
+
+    def copy(start, size, index):
+        return pltpu.make_async_copy(
+            grid_ref.at[pl.ds(start, size)], block_ref.at[pl.ds(start + 1, size)], sems.at[index]
+        )
+
+    for index in range(chunks):
+        copy(index * CHUNK, CHUNK, index).start()
+    copy(half_x, 2, chunks).start()
+    table = stencil_table()
+    block_ref[0] = jnp.zeros((BY, BZ), jnp.float32)
+    clear_rims(pass_refs, LOW_PLANES)
+    for level in range(1, LEVELS):
+        at = REST_AT[level] + high_from(level) * ROWS[level]
+        size = (COUNT[level] + 1 - high_from(level)) * ROWS[level]
+        stack_ref[pl.ds(at, size), :] = highs_ref[pl.ds(at, size), :]
+
+    def first_z(source, at, size):
+        both = apply_table(source[pl.ds(at, size), :], table)
+        first_ref[pl.ds(at, size), :] = both[:, :LANES]
+        end_ref[pl.ds(at, size), :] = both[:, LANES:]
+
+    def high_z(index, carry):
+        span = 5 * ROWS[0]
+        first_z(high_ref, aligned(low * ROWS[0] + index * span), span)
         return carry
 
-    lax.fori_loop(0, COUNT[0] // 8, first_z, 0)
-    last = COUNT[0] * ROWS[0]
-    both = apply_table(plane_ref[pl.ds(last, ROWS[0]), :], table)
-    first_ref[pl.ds(last, ROWS[0]), :] = both[:, :LANES]
-    end_ref[pl.ds(last, ROWS[0]), :] = both[:, LANES:]
+    lax.fori_loop(0, (COUNT[0] - low) // 5, high_z, 0)
+
+    def step(index, carry):
+        copy(index * CHUNK, CHUNK, index).wait()
+        planes = [index * (CHUNK // 2) + part for part in range(CHUNK // 2)]
+        first_planes(block_ref, pass_refs, plane_ref, planes, 0)
+        span = CHUNK // 2 * ROWS[0]
+        first_z(plane_ref, aligned(index * span), span)
+        return carry
+
+    lax.fori_loop(0, chunks, step, 0)
+    copy(half_x, 2, chunks).wait()
+    first_planes(block_ref, pass_refs, plane_ref, [low - 1], 0)
+    first_z(plane_ref, (low - 1) * ROWS[0], ROWS[0])
+    for level in range(1, LEVELS):
+
+        def load(plane, lanes, level=level):
+            if level == 1:
+                source = plane_ref if plane < low else high_ref
+                return source[pl.ds(plane * ROWS[0], ROWS[0]), lanes]
+            return stack_ref[pl.ds(REST_AT[level - 1] + plane * ROWS[level - 1], ROWS[level - 1]), lanes]
+
+        later_planes(level, range(high_from(level)), load, pass_refs, stack_ref)
     rest_ref[...] = apply_table(stack_ref[...], table[:, LANES:])
 
     def right_rows(level, plane):
         ref = end_ref if level == 0 else rest_ref
         at = (0 if level == 0 else REST_AT[level]) + plane * ROWS[level]
         return ref[pl.ds(at, ROWS[level]), :]
-
-    keep_x = sends(GX)
-    xface_ref[:, :LANES] = first_ref[pl.ds(last, ROWS[0]), :]
-    tile = jnp.where(iota((ROWS[0], LANES), 1) == END_AT, right_rows(0, COUNT[0]), 0.0)
-    xface_ref[:, LANES:] = tile
-    for level in range(1, LEVELS):
-        shape = (ROWS[level], LANES)
-        keep = tile_mask(level, shape) | (iota(shape, 1) == END_AT + level)
-        old = xface_ref[pl.ds(0, ROWS[level]), LANES:]
-        xface_ref[pl.ds(0, ROWS[level]), LANES:] = jnp.where(keep, right_rows(level, COUNT[level]), old)
-    xface_ref[...] = xface_ref[...] * keep_x
 
     yface_ref[:, :LANES] = first_ref[pl.ds(COUNT[0], COUNT[0], stride=ROWS[0]), :]
     yface_ref[:, LANES:] = jnp.zeros((COUNT[0], LANES), jnp.float32)
@@ -220,7 +317,6 @@
         old = yface_ref[pl.ds(0, size), LANES:]
         yface_ref[pl.ds(0, size), LANES:] = jnp.where(tile_mask(level, (size, LANES)), new, old)
 
-    total = None
     for level in range(LEVELS):
         lane = iota((ROWS[level], LANES), 1)
         face = jnp.zeros((ROWS[level], LANES), jnp.float32)
@@ -231,40 +327,36 @@
             if shift:
                 values = pltpu.roll(values, shift, 1)
             face = jnp.where(lane == target, values, face)
-        if total is None:
+        if level == 0:
             zface_ref[...] = face
-            total = True
         else:
             zface_ref[pl.ds(0, ROWS[level]), :] = zface_ref[pl.ds(0, ROWS[level]), :] + face
 
 
-def local_restriction(block):
+def low_half(block, high, highs):
     f32 = jnp.float32
-    scratch = [
-        pltpu.VMEM((BX + 1, BY, BZ), f32),
-        pltpu.VMEM((FIRST_ROWS, BZ), f32),
-        pltpu.VMEM((REST_ROWS, BZ), f32),
-        pltpu.VMEM((FIRST_ROWS, LANES), f32),
-        pltpu.SemaphoreType.DMA((BX // CHUNK,)),
-    ]
-    for level in range(LEVELS):
-        shape = ((COUNT[level] + 1) * PASS_ROWS[level], LANES)
-        scratch += [pltpu.VMEM(shape, f32), pltpu.VMEM(shape, f32)]
+    rows = COUNT[0] * ROWS[0]
     vmem = pl.BlockSpec(memory_space=pltpu.VMEM)
     return pl.pallas_call(
-        local_kernel,
+        low_kernel,
         out_shape=(
-            pltpu.VMEM((FIRST_ROWS, LANES), f32),
+            pltpu.VMEM((rows, LANES), f32),
             pltpu.VMEM((REST_ROWS, LANES), f32),
-            pltpu.VMEM((ROWS[0], BZ), f32),
             pltpu.VMEM((COUNT[0], BZ), f32),
             pltpu.VMEM((ROWS[0], LANES), f32),
         ),
-        in_specs=[pl.BlockSpec(memory_space=pl.ANY)],
-        out_specs=(vmem,) * 5,
-        scratch_shapes=scratch,
-        name="local_levels",
-    )(block)
+        in_specs=[pl.BlockSpec(memory_space=pl.ANY), vmem, vmem],
+        out_specs=(vmem,) * 4,
+        scratch_shapes=[
+            pltpu.VMEM((BX // 2 + 3, BY, BZ), f32),
+            pltpu.VMEM((high_from(0) * ROWS[0], BZ), f32),
+            pltpu.VMEM((REST_ROWS, BZ), f32),
+            pltpu.VMEM((rows, LANES), f32),
+            pltpu.SemaphoreType.DMA((BX // 2 // CHUNK + 1,)),
+        ]
+        + pass_scratch(LOW_PLANES),
+        name="low_half",
+    )(block, *resident(high, highs))
 
 
 def edge_kernel(xin_ref, yface_ref, zface_ref, yout_ref, zout_ref, yzout_ref):
@@ -424,8 +516,9 @@
 
 def per_device(residual_in):
     devices = lax.axis_size(GX_GY_GZ)
-    first, rest, xface, yface, zface = local_restriction(residual_in)
+    high, highs, xface = high_half(residual_in)
     xin = to_next(xface, GX)
+    first, rest, yface, zface = low_half(residual_in, high, highs)
     yface, zface, edge = add_edges(xin, yface, zface)
     yin, zin, edgein = to_next(yface, GY), to_next(zface, GZ), to_next(edge, GY, GZ)
     *levels, sums = finish_levels(first, rest, xin, yin, zin, edgein, devices)

time: 45 us -> 42.9 us (0.953)
  waiting for transfers between devices: 6 us -> 3.35 us
  Pallas kernels: 5.39 us -> 5.91 us
    ppermute x4, waiting for transfers between devices: 6 us -> 3.35 us  [to_next(): return lax.ppermute(face, sum(axes, ()), route)]
    pallas_call x1 -> x2, Pallas kernels: 4.01 us -> 4.53 us  [the longest x1 2.64 us: low_half(): pl.pallas_call(low_kernel, out_shape=(pltpu.VMEM((rows, LANES), f32), plt...]
  transfers between devices with their start and end apart: 4 -> 4, of which waited for: 3 -> 2; matrix products, arithmetic and copies ran while one was open for 0% -> 0% of each run, Pallas kernels for 0% -> 6%
where the time goes in v3:
time: 42.9 us; the launch traced here: 42.8 us
  blocking collectives  24.2 us (56%)
  starting transfers between devices  8.68 us (20%)
  Pallas kernels  5.91 us (14%)
  waiting for transfers between devices  3.35 us (8%)
  between operations  0.67 us (2%)
    all_to_all x1, blocking collectives, per_device(): sums = lax.all_to_all(sums, GX_GY_GZ, 0, 0, tiled=True)  24.2 us
    ppermute x4, starting transfers between devices, to_next(): return lax.ppermute(face, sum(axes, ()), route)  8.68 us
    ppermute x4, waiting for transfers between devices, to_next(): return lax.ppermute(face, sum(axes, ()), route)  3.35 us
    pallas_call x1, Pallas kernels, low_half(): pl.pallas_call(low_kernel, out_shape=(pltpu.VMEM((rows, LANES), f32), plt...  2.64 us
    pallas_call x1, Pallas kernels, high_half(): pl.pallas_call(high_kernel, out_shape=(pltpu.VMEM((FIRST_ROWS, BZ), f32),...  1.9 us
    pallas_call x1, Pallas kernels, scale_levels(): pl.pallas_call(scale_kernel, out_shape=tuple((jax.ShapeDtypeStruct(shape,...  1.01 us
  transfers between devices with their start and end apart: 4, of which 2 were waited for; matrix products, arithmetic and copies ran while one was open for 0% of the time, Pallas kernels for 6%

profile of v3, /device:TPU:1, one launch (start us, length us, event | category | flops | bytes accessed | tf_op | source)
XLA Modules:
  0.0 42.8 jit_solution(7284207857597176981)
XLA Ops:
  0.6 1.9 %high_half.1 = (f32[1320,256]{1,0:T(8,128)S(1)}, f32[616,256]{1,0:T(8,128)S(1)}, f32[40,256]{1,0:T(8,128)S(1)}) custom-call(f32[64,64,256]{2,1,0:T(8,128)} %grid_ref.3), custom_call_target="tpu_custom_call" | custom-call | tf_op jit(solution)/shard_map/high_half/pallas_call | solution.py:223
  2.5 2.1 %collective-permute-start = (f32[40,256]{1,0:T(8,128)S(1)}, f32[40,256]{1,0:T(8,128)S(1)}, u32[]{:S(2)}, u32[]{:S(2)}) collective-permute-start(f32[40,256]{1,0:T(8,128)S(1)} %get-tuple-element.26), channel_id=1, source_target_pairs={{0,64},{64,128},{128,192},{192,0},{1,65},{65,129},{129,193},{193,1... | collective-permute-start | bytes 122888 | tf_op jit(solution)/shard_map/ppermute | solution.py:514
  4.6 2.6 %low_half.1 = (f32[1280,128]{1,0:T(8,128)S(1)}, f32[616,128]{1,0:T(8,128)S(1)}, f32[32,256]{1,0:T(8,128)S(1)}, f32[40,128]{1,0:T(8,128)S(1)}) custom-call(f32[64,64,256]{2,1,0:T(8,128)} %grid_ref.3, f32[1320,256]{1,0:T(8,128)S(1)} %get-tuple-element.22.high_ref, f32[616,256]{1,0:T(8,128)S(1)} %get-tuple-element.23.highs_ref), custom_call_target="tpu_custom_call" | custom-call | tf_op jit(solution)/shard_map/low_half/pallas_call | solution.py:340
  7.3 0.0 collective-permute-done.xin_ref
  7.3 3.2 %collective-permute-start.1 = (f32[32,256]{1,0:T(8,128)S(1)}, f32[32,256]{1,0:T(8,128)S(1)}, u32[]{:S(2)}, u32[]{:S(2)}) collective-permute-start(f32[32,256]{1,0:T(8,128)S(1)} %get-tuple-element.29), channel_id=1, source_target_pairs={{0,8},{8,16},{16,24},{24,32},{32,40},{40,48},{48,56},{56,0},{1,9},... | collective-permute-start | bytes 98312 | tf_op jit(solution)/shard_map/ppermute | solution.py:514
  10.5 1.6 %collective-permute-start.2 = (f32[32,128]{1,0:T(8,128)S(1)}, f32[32,128]{1,0:T(8,128)S(1)}, u32[]{:S(2)}, u32[]{:S(2)}) collective-permute-start(f32[32,128]{1,0:T(8,128)S(1)} %get-tuple-element.30), channel_id=1, source_target_pairs={{0,1},{1,2},{2,3},{3,4},{4,5},{5,6},{6,7},{7,0},{8,9},{9,10},{10,1... | collective-permute-start | bytes 49160 | tf_op jit(solution)/shard_map/ppermute | solution.py:514
  12.2 1.7 %collective-permute-start.3 = (f32[8,128]{1,0:T(8,128)S(1)}, f32[8,128]{1,0:T(8,128)S(1)}, u32[]{:S(2)}, u32[]{:S(2)}) collective-permute-start(f32[8,128]{1,0:T(8,128)S(1)} %get-tuple-element.31), channel_id=1, source_target_pairs={{0,9},{1,10},{2,11},{3,12},{4,13},{5,14},{6,15},{7,8},{8,17},{9,18... | collective-permute-start | bytes 12296 | tf_op jit(solution)/shard_map/ppermute | solution.py:514
  13.9 2.7 %collective-permute-done.3.yzin_ref = f32[8,128]{1,0:T(8,128)S(1)} collective-permute-done((f32[8,128]{1,0:T(8,128)S(1)}, f32[8,128]{1,0:T(8,128)S(1)}, u32[]{:S(2)}, u32[]{:S(2)}) %collective-permute-start.3) | collective-permute-done | bytes 4128 | tf_op jit(solution)/shard_map/ppermute | solution.py:514
  16.6 0.6 %collective-permute-done.2.zin_ref = f32[32,128]{1,0:T(8,128)S(1)} collective-permute-done((f32[32,128]{1,0:T(8,128)S(1)}, f32[32,128]{1,0:T(8,128)S(1)}, u32[]{:S(2)}, u32[]{:S(2)}) %collective-permute-start.2) | collective-permute-done | bytes 16416 | tf_op jit(solution)/shard_map/ppermute | solution.py:514
  17.2 0.0 collective-permute-done.1.yin_ref
  17.2 0.3 finish.1
  17.6 24.2 %all_to_all.11 = f32[256,1,128]{2,1,0:T(1,128)S(1)} all-to-all(f32[256,1,128]{2,1,0:T(1,128)S(1)} %bitcast.5), channel_id=1, replica_groups=mesh['gx'=4,'gy_0'=4,'gy_1'=2,'gz'=8] {'gx','gy_0','gy_1','gz'}, dimensions={0} | all-to-all | bytes 262144 | tf_op jit(solution)/shard_map/all_to_all | solution.py:525
  41.8 1.0 %scale.1 = (f32[32,32,128]{2,1,0:T(8,128)}, f32[16,16,64]{2,1,0:T(8,128)}, f32[8,8,32]{2,1,0:T(8,128)}, f32[4,4,16]{2,1,0:T(4,128)}, f32[2,2,8]{2,1,0:T(2,128)}, /*index=5*/f32[5]{0:T(128)}) custom-call(f32[256,128]{1,0:T(8,128)S(1)} %bitcast.4, f32[32,32,128]{2,1,0:T(8,128)S(1)} %get-tuple-element.33.refs_0_, f32[16,16,128]{2,1,0:T(8,128)S(1)} %get-tuple-element.34.refs_1_, ...), custom_call_target="tpu_custom_call" | custom-call | tf_op jit(solution)/shard_map/scale/pallas_call | solution.py:495
  (1 shorter events, 0.0 us)
Async XLA Ops:
  2.5 4.8 %collective-permute-start = (f32[40,256]{1,0:T(8,128)S(1)}, f32[40,256]{1,0:T(8,128)S(1)}, u32[]{:S(2)}, u32[]{:S(2)}) collective-permute-start(f32[40,256]{1,0:T(8,128)S(1)} %get-tuple-element.26), channel_id=1, source_target_pairs={{0,64},{64,128},{128,192},{192,0},{1,65},{65,129},{129,193},{193,1... | collective-permute-start | bytes 122888 | tf_op jit(solution)/shard_map/ppermute | solution.py:514
  7.3 9.9 %collective-permute-start.1 = (f32[32,256]{1,0:T(8,128)S(1)}, f32[32,256]{1,0:T(8,128)S(1)}, u32[]{:S(2)}, u32[]{:S(2)}) collective-permute-start(f32[32,256]{1,0:T(8,128)S(1)} %get-tuple-element.29), channel_id=1, source_target_pairs={{0,8},{8,16},{16,24},{24,32},{32,40},{40,48},{48,56},{56,0},{1,9},... | collective-permute-start | bytes 98312 | tf_op jit(solution)/shard_map/ppermute | solution.py:514
  10.5 6.7 %collective-permute-start.2 = (f32[32,128]{1,0:T(8,128)S(1)}, f32[32,128]{1,0:T(8,128)S(1)}, u32[]{:S(2)}, u32[]{:S(2)}) collective-permute-start(f32[32,128]{1,0:T(8,128)S(1)} %get-tuple-element.30), channel_id=1, source_target_pairs={{0,1},{1,2},{2,3},{3,4},{4,5},{5,6},{6,7},{7,0},{8,9},{9,10},{10,1... | collective-permute-start | bytes 49160 | tf_op jit(solution)/shard_map/ppermute | solution.py:514
  12.2 4.5 %collective-permute-start.3 = (f32[8,128]{1,0:T(8,128)S(1)}, f32[8,128]{1,0:T(8,128)S(1)}, u32[]{:S(2)}, u32[]{:S(2)}) collective-permute-start(f32[8,128]{1,0:T(8,128)S(1)} %get-tuple-element.31), channel_id=1, source_target_pairs={{0,9},{1,10},{2,11},{3,12},{4,13},{5,14},{6,15},{7,8},{8,17},{9,18... | collective-permute-start | bytes 12296 | tf_op jit(solution)/shard_map/ppermute | solution.py:514

commit v4 on v3

--- a/solution.py
+++ b/solution.py
@@ -29,6 +29,7 @@
 LANE_AT = [0, 0, 64, 96, 112]
 LANE_COUNT = [128, 64, 32, 16, 8]
 END_AT = 120
+SPARE = 125
 FACE_AT = [-1, 30, 45, 52, 55]
 
 
@@ -202,7 +203,6 @@
     for level in range(1, LEVELS):
         parts.append(stack_ref[pl.ds(REST_AT[level] + COUNT[level] * ROWS[level], ROWS[level]), :])
     faces = apply_table(jnp.concatenate(parts, axis=0), table) * keep_x
-    xface_ref[:, :LANES] = faces[: ROWS[0], :LANES]
     tiles = [jnp.where(iota((ROWS[0], LANES), 1) == END_AT, faces[: ROWS[0], LANES:], 0.0)]
     at = ROWS[0]
     for level in range(1, LEVELS):
@@ -214,7 +214,17 @@
             blank = jnp.zeros((ROWS[0] - ROWS[level], LANES), jnp.float32)
             face = jnp.concatenate([face, blank], axis=0)
         tiles.append(face)
-    xface_ref[:, LANES:] = sum(tiles[1:], tiles[0])
+    tile = sum(tiles[1:], tiles[0])
+    xface_ref[pl.ds(0, 32), :] = faces[:32, :LANES]
+    lane = iota((16, LANES), 1)
+    spare = pltpu.roll(jnp.where(lane == END_AT, tile[16:32], 0.0), SPARE - END_AT, 1)
+    xface_ref[pl.ds(32, 16), :] = tile[:16] + spare
+    lane = iota((1, LANES), 1)
+    row = iota((8, LANES), 0)
+    second = jnp.where(lane == END_AT, tile[32:33], tile[16:17])
+    xface_ref[pl.ds(48, 8), :] = jnp.where(
+        row == 0, faces[32:33, :LANES], jnp.where(row == 1, second, 0.0)
+    )
 
 
 def high_half(block):
@@ -225,7 +235,7 @@
         out_shape=(
             pltpu.VMEM((FIRST_ROWS, BZ), f32),
             pltpu.VMEM((REST_ROWS, BZ), f32),
-            pltpu.VMEM((ROWS[0], BZ), f32),
+            pltpu.VMEM((56, LANES), f32),
         ),
         in_specs=[pl.BlockSpec(memory_space=pl.ANY)],
         out_specs=(vmem,) * 3,
@@ -301,8 +311,8 @@
         at = (0 if level == 0 else REST_AT[level]) + plane * ROWS[level]
         return ref[pl.ds(at, ROWS[level]), :]
 
-    yface_ref[:, :LANES] = first_ref[pl.ds(COUNT[0], COUNT[0], stride=ROWS[0]), :]
-    yface_ref[:, LANES:] = jnp.zeros((COUNT[0], LANES), jnp.float32)
+    yface_ref[pl.ds(0, 32), :] = first_ref[pl.ds(COUNT[0], COUNT[0], stride=ROWS[0]), :]
+    yface_ref[pl.ds(32, 16), :] = jnp.zeros((16, LANES), jnp.float32)
     for level in range(1, LEVELS):
         count = COUNT[level]
         at = REST_AT[level] + count
@@ -314,8 +324,8 @@
                 row = rest_ref[pl.ds(at + plane * ROWS[level], 1), :]
                 new = jnp.where(iota((8, LANES), 0) == plane, row, new)
         size = max(count, 8)
-        old = yface_ref[pl.ds(0, size), LANES:]
-        yface_ref[pl.ds(0, size), LANES:] = jnp.where(tile_mask(level, (size, LANES)), new, old)
+        old = yface_ref[pl.ds(32, size), :]
+        yface_ref[pl.ds(32, size), :] = jnp.where(tile_mask(level, (size, LANES)), new, old)
 
     for level in range(LEVELS):
         lane = iota((ROWS[level], LANES), 1)
@@ -342,7 +352,7 @@
         out_shape=(
             pltpu.VMEM((rows, LANES), f32),
             pltpu.VMEM((REST_ROWS, LANES), f32),
-            pltpu.VMEM((COUNT[0], BZ), f32),
+            pltpu.VMEM((48, LANES), f32),
             pltpu.VMEM((ROWS[0], LANES), f32),
         ),
         in_specs=[pl.BlockSpec(memory_space=pl.ANY), vmem, vmem],
@@ -361,23 +371,32 @@
 
 def edge_kernel(xin_ref, yface_ref, zface_ref, yout_ref, zout_ref, yzout_ref):
     count = COUNT[0]
-    lane = iota((ROWS[0], LANES), 1)
-    zface = zface_ref[...] + jnp.where(lane >= END_AT, xin_ref[:, LANES:], 0.0)
     keep_y = sends(GY)
     keep_z = sends(GZ)
+    lane = iota((16, LANES), 1)
+    top = xin_ref[pl.ds(32, 16), :]
+    ends = (lane >= END_AT) & (lane < END_AT + LEVELS)
+    spare = pltpu.roll(top, LANES + END_AT - SPARE, 1)
+    second = xin_ref[pl.ds(49, 1), :]
+    last = iota((1, LANES), 1)
+    middle = jnp.where(lane == END_AT, spare, 0.0) + jnp.where(
+        (iota((16, LANES), 0) == 0) & (lane == END_AT + 1), second, 0.0
+    )
+    bottom = jnp.where((iota((8, LANES), 0) == 0) & (last == END_AT), second, 0.0)
+    zface = zface_ref[...] + jnp.concatenate([jnp.where(ends, top, 0.0), middle, bottom], axis=0)
     zout_ref[...] = zface[:count] * keep_z
-    row = iota((count, LANES), 0)
-    yout_ref[:, :LANES] = (
-        yface_ref[:, :LANES] + jnp.where(row == 0, xin_ref[pl.ds(count, 1), :LANES], 0.0)
-    ) * keep_y
     edge = jnp.zeros((1, LANES), jnp.float32)
     corner = jnp.zeros((1, LANES), jnp.float32)
     for level in range(LEVELS):
         at = COUNT[level]
         if level:
-            edge = jnp.where(tile_mask(level, (1, LANES)), xin_ref[pl.ds(at, 1), LANES:], edge)
+            source = second if level == 1 else top[at : at + 1]
+            edge = jnp.where(tile_mask(level, (1, LANES)), source, edge)
         corner = jnp.where(face_mask(level, (1, LANES)), zface[at : at + 1], corner)
-    yout_ref[:, LANES:] = (yface_ref[:, LANES:] + jnp.where(row == 0, edge, 0.0)) * keep_y
+    added = jnp.where(iota((count, LANES), 0) == 0, xin_ref[pl.ds(48, 1), :], 0.0)
+    yout_ref[pl.ds(0, count), :] = (yface_ref[pl.ds(0, count), :] + added) * keep_y
+    added = jnp.where(iota((16, LANES), 0) == 0, edge, 0.0)
+    yout_ref[pl.ds(count, 16), :] = (yface_ref[pl.ds(count, 16), :] + added) * keep_y
     yzout_ref[...] = jnp.where(iota((8, LANES), 0) == 0, corner, 0.0) * (keep_y * keep_z)
 
 
@@ -398,7 +417,7 @@
     return pl.pallas_call(
         edge_kernel,
         out_shape=(
-            pltpu.VMEM((COUNT[0], BZ), f32),
+            pltpu.VMEM((48, LANES), f32),
             pltpu.VMEM((COUNT[0], LANES), f32),
             pltpu.VMEM((8, LANES), f32),
         ),
@@ -416,7 +435,7 @@
     for level in range(LEVELS):
         count = COUNT[level]
         rows = max(count, 8)
-        half = slice(0, LANES) if level == 0 else slice(LANES, 2 * LANES)
+        face_at = 32 if level else 0
         source = first_ref if level == 0 else rest_ref
         shape = (rows, LANES)
         inside = tile_mask(level, shape) & (iota(shape, 0) < count)
@@ -426,8 +445,8 @@
             at = REST_AT[level] + plane * ROWS[level]
             values = source[pl.ds(at, rows), :]
             if plane == 0:
-                values = values + xin_ref[pl.ds(0, rows), half]
-            yrow = jnp.where(iota((8, LANES), 0) == 0, yin_ref[pl.ds(plane, 1), half], 0.0)
+                values = values + xin_ref[pl.ds(face_at, rows), :]
+            yrow = jnp.where(iota((8, LANES), 0) == 0, yin_ref[pl.ds(face_at + plane, 1), :], 0.0)
             if rows > 8:
                 yrow = jnp.concatenate([yrow, jnp.zeros((rows - 8, LANES), jnp.float32)], axis=0)
             shift = (LANE_AT[level] - face_lane(level, plane)) % LANES
@@ -520,7 +539,9 @@
     xin = to_next(xface, GX)
     first, rest, yface, zface = low_half(residual_in, high, highs)
     yface, zface, edge = add_edges(xin, yface, zface)
-    yin, zin, edgein = to_next(yface, GY), to_next(zface, GZ), to_next(edge, GY, GZ)
+    edgein = to_next(edge, GY, GZ)
+    zin = to_next(zface, GZ)
+    yin = to_next(yface, GY)
     *levels, sums = finish_levels(first, rest, xin, yin, zin, edgein, devices)
     sums = lax.all_to_all(sums, GX_GY_GZ, 0, 0, tiled=True)
     return tuple(scale_levels(sums, levels))

time: 42.9 us -> 42.9 us (level)
  no operation moved by 1% of the time
where the time goes in v4:
time: 42.9 us; the launch traced here: 42.7 us
  blocking collectives  24.2 us (56%)
  starting transfers between devices  8.53 us (20%)
  Pallas kernels  5.99 us (14%)
  waiting for transfers between devices  3.35 us (8%)
  between operations  0.67 us (2%)
    all_to_all x1, blocking collectives, per_device(): sums = lax.all_to_all(sums, GX_GY_GZ, 0, 0, tiled=True)  24.2 us
    ppermute x4, starting transfers between devices, to_next(): return lax.ppermute(face, sum(axes, ()), route)  8.53 us
    ppermute x4, waiting for transfers between devices, to_next(): return lax.ppermute(face, sum(axes, ()), route)  3.35 us
    pallas_call x1, Pallas kernels, low_half(): pl.pallas_call(low_kernel, out_shape=(pltpu.VMEM((rows, LANES), f32), plt...  2.64 us
    pallas_call x1, Pallas kernels, high_half(): pl.pallas_call(high_kernel, out_shape=(pltpu.VMEM((FIRST_ROWS, BZ), f32),...  1.91 us
    pallas_call x1, Pallas kernels, scale_levels(): pl.pallas_call(scale_kernel, out_shape=tuple((jax.ShapeDtypeStruct(shape,...  1.01 us
  transfers between devices with their start and end apart: 4, of which 2 were waited for; matrix products, arithmetic and copies ran while one was open for 0% of the time, Pallas kernels for 6%

profile of v4, /device:TPU:1, one launch (start us, length us, event | category | flops | bytes accessed | tf_op | source)
XLA Modules:
  0.0 42.7 jit_solution(9065223825064647861)
XLA Ops:
  0.6 1.9 %high_half.1 = (f32[1320,256]{1,0:T(8,128)S(1)}, f32[616,256]{1,0:T(8,128)S(1)}, f32[56,128]{1,0:T(8,128)S(1)}) custom-call(f32[64,64,256]{2,1,0:T(8,128)} %grid_ref.3), custom_call_target="tpu_custom_call" | custom-call | tf_op jit(solution)/shard_map/high_half/pallas_call | solution.py:233
  2.5 2.1 %collective-permute-start = (f32[56,128]{1,0:T(8,128)S(1)}, f32[56,128]{1,0:T(8,128)S(1)}, u32[]{:S(2)}, u32[]{:S(2)}) collective-permute-start(f32[56,128]{1,0:T(8,128)S(1)} %get-tuple-element.26), channel_id=1, source_target_pairs={{0,64},{64,128},{128,192},{192,0},{1,65},{65,129},{129,193},{193,1... | collective-permute-start | bytes 86024 | tf_op jit(solution)/shard_map/ppermute | solution.py:533
  4.7 2.6 %low_half.1 = (f32[1280,128]{1,0:T(8,128)S(1)}, f32[616,128]{1,0:T(8,128)S(1)}, f32[48,128]{1,0:T(8,128)S(1)}, f32[40,128]{1,0:T(8,128)S(1)}) custom-call(f32[64,64,256]{2,1,0:T(8,128)} %grid_ref.3, f32[1320,256]{1,0:T(8,128)S(1)} %get-tuple-element.22.high_ref, f32[616,256]{1,0:T(8,128)S(1)} %get-tuple-element.23.highs_ref), custom_call_target="tpu_custom_call" | custom-call | tf_op jit(solution)/shard_map/low_half/pallas_call | solution.py:350
  7.3 0.0 collective-permute-done.xin_ref
  7.3 0.1 edges.1
  7.4 3.1 %collective-permute-start.1 = (f32[48,128]{1,0:T(8,128)S(1)}, f32[48,128]{1,0:T(8,128)S(1)}, u32[]{:S(2)}, u32[]{:S(2)}) collective-permute-start(f32[48,128]{1,0:T(8,128)S(1)} %get-tuple-element.29), channel_id=1, source_target_pairs={{0,8},{8,16},{16,24},{24,32},{32,40},{40,48},{48,56},{56,0},{1,9},... | collective-permute-start | bytes 73736 | tf_op jit(solution)/shard_map/ppermute | solution.py:533
  10.5 1.6 %collective-permute-start.2 = (f32[32,128]{1,0:T(8,128)S(1)}, f32[32,128]{1,0:T(8,128)S(1)}, u32[]{:S(2)}, u32[]{:S(2)}) collective-permute-start(f32[32,128]{1,0:T(8,128)S(1)} %get-tuple-element.30), channel_id=1, source_target_pairs={{0,1},{1,2},{2,3},{3,4},{4,5},{5,6},{6,7},{7,0},{8,9},{9,10},{10,1... | collective-permute-start | bytes 49160 | tf_op jit(solution)/shard_map/ppermute | solution.py:533
  12.1 1.7 %collective-permute-start.3 = (f32[8,128]{1,0:T(8,128)S(1)}, f32[8,128]{1,0:T(8,128)S(1)}, u32[]{:S(2)}, u32[]{:S(2)}) collective-permute-start(f32[8,128]{1,0:T(8,128)S(1)} %get-tuple-element.31), channel_id=1, source_target_pairs={{0,9},{1,10},{2,11},{3,12},{4,13},{5,14},{6,15},{7,8},{8,17},{9,18... | collective-permute-start | bytes 12296 | tf_op jit(solution)/shard_map/ppermute | solution.py:533
  13.8 2.7 %collective-permute-done.3.yzin_ref = f32[8,128]{1,0:T(8,128)S(1)} collective-permute-done((f32[8,128]{1,0:T(8,128)S(1)}, f32[8,128]{1,0:T(8,128)S(1)}, u32[]{:S(2)}, u32[]{:S(2)}) %collective-permute-start.3) | collective-permute-done | bytes 4128 | tf_op jit(solution)/shard_map/ppermute | solution.py:533
  16.5 0.6 %collective-permute-done.2.zin_ref = f32[32,128]{1,0:T(8,128)S(1)} collective-permute-done((f32[32,128]{1,0:T(8,128)S(1)}, f32[32,128]{1,0:T(8,128)S(1)}, u32[]{:S(2)}, u32[]{:S(2)}) %collective-permute-start.2) | collective-permute-done | bytes 16416 | tf_op jit(solution)/shard_map/ppermute | solution.py:533
  17.2 0.0 collective-permute-done.1.yin_ref
  17.2 0.3 finish.1
  17.5 24.2 %all_to_all.11 = f32[256,1,128]{2,1,0:T(1,128)S(1)} all-to-all(f32[256,1,128]{2,1,0:T(1,128)S(1)} %bitcast.5), channel_id=1, replica_groups=mesh['gx'=4,'gy_0'=4,'gy_1'=2,'gz'=8] {'gx','gy_0','gy_1','gz'}, dimensions={0} | all-to-all | bytes 262144 | tf_op jit(solution)/shard_map/all_to_all | solution.py:546
  41.7 1.0 %scale.1 = (f32[32,32,128]{2,1,0:T(8,128)}, f32[16,16,64]{2,1,0:T(8,128)}, f32[8,8,32]{2,1,0:T(8,128)}, f32[4,4,16]{2,1,0:T(4,128)}, f32[2,2,8]{2,1,0:T(2,128)}, /*index=5*/f32[5]{0:T(128)}) custom-call(f32[256,128]{1,0:T(8,128)S(1)} %bitcast.4, f32[32,32,128]{2,1,0:T(8,128)S(1)} %get-tuple-element.33.refs_0_, f32[16,16,128]{2,1,0:T(8,128)S(1)} %get-tuple-element.34.refs_1_, ...), custom_call_target="tpu_custom_call" | custom-call | tf_op jit(solution)/shard_map/scale/pallas_call | solution.py:514
Async XLA Ops:
  2.5 4.8 %collective-permute-start = (f32[56,128]{1,0:T(8,128)S(1)}, f32[56,128]{1,0:T(8,128)S(1)}, u32[]{:S(2)}, u32[]{:S(2)}) collective-permute-start(f32[56,128]{1,0:T(8,128)S(1)} %get-tuple-element.26), channel_id=1, source_target_pairs={{0,64},{64,128},{128,192},{192,0},{1,65},{65,129},{129,193},{193,1... | collective-permute-start | bytes 86024 | tf_op jit(solution)/shard_map/ppermute | solution.py:533
  7.4 9.8 %collective-permute-start.1 = (f32[48,128]{1,0:T(8,128)S(1)}, f32[48,128]{1,0:T(8,128)S(1)}, u32[]{:S(2)}, u32[]{:S(2)}) collective-permute-start(f32[48,128]{1,0:T(8,128)S(1)} %get-tuple-element.29), channel_id=1, source_target_pairs={{0,8},{8,16},{16,24},{24,32},{32,40},{40,48},{48,56},{56,0},{1,9},... | collective-permute-start | bytes 73736 | tf_op jit(solution)/shard_map/ppermute | solution.py:533
  10.5 6.7 %collective-permute-start.2 = (f32[32,128]{1,0:T(8,128)S(1)}, f32[32,128]{1,0:T(8,128)S(1)}, u32[]{:S(2)}, u32[]{:S(2)}) collective-permute-start(f32[32,128]{1,0:T(8,128)S(1)} %get-tuple-element.30), channel_id=1, source_target_pairs={{0,1},{1,2},{2,3},{3,4},{4,5},{5,6},{6,7},{7,0},{8,9},{9,10},{10,1... | collective-permute-start | bytes 49160 | tf_op jit(solution)/shard_map/ppermute | solution.py:533
  12.1 4.4 %collective-permute-start.3 = (f32[8,128]{1,0:T(8,128)S(1)}, f32[8,128]{1,0:T(8,128)S(1)}, u32[]{:S(2)}, u32[]{:S(2)}) collective-permute-start(f32[8,128]{1,0:T(8,128)S(1)} %get-tuple-element.31), channel_id=1, source_target_pairs={{0,9},{1,10},{2,11},{3,12},{4,13},{5,14},{6,15},{7,8},{8,17},{9,18... | collective-permute-start | bytes 12296 | tf_op jit(solution)/shard_map/ppermute | solution.py:533

commit v5 on v4

--- a/solution.py
+++ b/solution.py
@@ -18,6 +18,7 @@
 BX, BY, BZ = 64, 64, 256
 LANES = 128
 CHUNK = 8
+LOW_CHUNK = 16
 COUNT = [BX >> level for level in range(1, LEVELS + 1)]
 ROWS = [40, 24, 16, 8, 8]
 PASS_ROWS = [88, 56, 40, 24, 24]
@@ -71,10 +72,10 @@
 
 
 def apply_table(values, table):
-    high = values.astype(jnp.bfloat16)
-    low = (values - high.astype(jnp.float32)).astype(jnp.bfloat16)
-    top = jnp.dot(high, table, preferred_element_type=jnp.float32)
-    return top + jnp.dot(low, table, preferred_element_type=jnp.float32)
+    left = values - values.astype(jnp.bfloat16).astype(jnp.float32)
+    both = jnp.concatenate([values, left], axis=0).astype(jnp.bfloat16)
+    out = jnp.dot(both, table, preferred_element_type=jnp.float32)
+    return out[: values.shape[0]] + out[values.shape[0] :]
 
 
 def aligned(start):
@@ -252,7 +253,7 @@
     block_ref, plane_ref, stack_ref, end_ref, sems = scratch[:5]
     pass_refs = scratch[5:]
     half_x = BX // 2
-    chunks = half_x // CHUNK
+    chunks = half_x // LOW_CHUNK
     low = high_from(0)
 
     def copy(start, size, index):
@@ -261,7 +262,7 @@
         )
 
     for index in range(chunks):
-        copy(index * CHUNK, CHUNK, index).start()
+        copy(index * LOW_CHUNK, LOW_CHUNK, index).start()
     copy(half_x, 2, chunks).start()
     table = stencil_table()
     block_ref[0] = jnp.zeros((BY, BZ), jnp.float32)
@@ -284,10 +285,10 @@
     lax.fori_loop(0, (COUNT[0] - low) // 5, high_z, 0)
 
     def step(index, carry):
-        copy(index * CHUNK, CHUNK, index).wait()
-        planes = [index * (CHUNK // 2) + part for part in range(CHUNK // 2)]
+        copy(index * LOW_CHUNK, LOW_CHUNK, index).wait()
+        planes = [index * (LOW_CHUNK // 2) + part for part in range(LOW_CHUNK // 2)]
         first_planes(block_ref, pass_refs, plane_ref, planes, 0)
-        span = CHUNK // 2 * ROWS[0]
+        span = LOW_CHUNK // 2 * ROWS[0]
         first_z(plane_ref, aligned(index * span), span)
         return carry
 
@@ -362,7 +363,7 @@
             pltpu.VMEM((high_from(0) * ROWS[0], BZ), f32),
             pltpu.VMEM((REST_ROWS, BZ), f32),
             pltpu.VMEM((rows, LANES), f32),
-            pltpu.SemaphoreType.DMA((BX // 2 // CHUNK + 1,)),
+            pltpu.SemaphoreType.DMA((BX // 2 // LOW_CHUNK + 1,)),
         ]
         + pass_scratch(LOW_PLANES),
         name="low_half",
@@ -486,15 +487,16 @@
     devices = sums_ref.shape[0]
     totals = jnp.sum(sums_ref[...], axis=0, keepdims=True)
     lane = iota((1, LANES), 1)
-    product = jnp.ones((1, 1), jnp.float32)
+    square = jnp.ones((1, 1), jnp.float32)
     scales = jnp.zeros((1, LANES), jnp.float32)
     for level in range(LEVELS):
         cells = COUNT[level] * COUNT[level] * LANE_COUNT[level] * devices
-        total = jnp.sum(jnp.where(lane == level, totals, 0.0), axis=1, keepdims=True)
-        scale = jnp.sqrt(total / (product * product) * (1.0 / cells) + EPSILON)
-        product = product * scale
+        mean = jnp.sum(jnp.where(lane == level, totals, 0.0), axis=1, keepdims=True) * (1.0 / cells)
+        before = square
+        square = mean + EPSILON * before
+        scale = jnp.sqrt(square / before)
         scales = jnp.where(lane == level, scale, scales)
-        factor = jnp.broadcast_to(1.0 / product, (8, LANES))
+        factor = jnp.broadcast_to(1.0 / jnp.sqrt(square), (8, LANES))
         count = COUNT[level]
         for plane in range(count):
             for tile in range(max(count // 8, 1)):

time: 42.9 us -> 42.9 us (level)
  no operation moved by 1% of the time
where the time goes in v5:
time: 42.9 us; the launch traced here: 42.7 us
  blocking collectives  24.2 us (56%)
  starting transfers between devices  8.66 us (20%)
  Pallas kernels  5.83 us (14%)
  waiting for transfers between devices  3.38 us (8%)
  between operations  0.66 us (2%)
    all_to_all x1, blocking collectives, per_device(): sums = lax.all_to_all(sums, GX_GY_GZ, 0, 0, tiled=True)  24.2 us
    ppermute x4, starting transfers between devices, to_next(): return lax.ppermute(face, sum(axes, ()), route)  8.66 us
    ppermute x4, waiting for transfers between devices, to_next(): return lax.ppermute(face, sum(axes, ()), route)  3.38 us
    pallas_call x1, Pallas kernels, low_half(): pl.pallas_call(low_kernel, out_shape=(pltpu.VMEM((rows, LANES), f32), plt...  2.49 us
    pallas_call x1, Pallas kernels, high_half(): pl.pallas_call(high_kernel, out_shape=(pltpu.VMEM((FIRST_ROWS, BZ), f32),...  1.91 us
    pallas_call x1, Pallas kernels, scale_levels(): pl.pallas_call(scale_kernel, out_shape=tuple((jax.ShapeDtypeStruct(shape,...  1.01 us
  transfers between devices with their start and end apart: 4, of which 2 were waited for; matrix products, arithmetic and copies ran while one was open for 0% of the time, Pallas kernels for 6%

profile of v5, /device:TPU:1, one launch (start us, length us, event | category | flops | bytes accessed | tf_op | source)
XLA Modules:
  0.0 42.7 jit_solution(13859800828805513338)
XLA Ops:
  0.6 1.9 %high_half.1 = (f32[1320,256]{1,0:T(8,128)S(1)}, f32[616,256]{1,0:T(8,128)S(1)}, f32[56,128]{1,0:T(8,128)S(1)}) custom-call(f32[64,64,256]{2,1,0:T(8,128)} %grid_ref.3), custom_call_target="tpu_custom_call" | custom-call | tf_op jit(solution)/shard_map/high_half/pallas_call | solution.py:234
  2.5 2.1 %collective-permute-start = (f32[56,128]{1,0:T(8,128)S(1)}, f32[56,128]{1,0:T(8,128)S(1)}, u32[]{:S(2)}, u32[]{:S(2)}) collective-permute-start(f32[56,128]{1,0:T(8,128)S(1)} %get-tuple-element.26), channel_id=1, source_target_pairs={{0,64},{64,128},{128,192},{192,0},{1,65},{65,129},{129,193},{193,1... | collective-permute-start | bytes 86024 | tf_op jit(solution)/shard_map/ppermute | solution.py:535
  4.7 2.5 %low_half.1 = (f32[1280,128]{1,0:T(8,128)S(1)}, f32[616,128]{1,0:T(8,128)S(1)}, f32[48,128]{1,0:T(8,128)S(1)}, f32[40,128]{1,0:T(8,128)S(1)}) custom-call(f32[64,64,256]{2,1,0:T(8,128)} %grid_ref.3, f32[1320,256]{1,0:T(8,128)S(1)} %get-tuple-element.22.high_ref, f32[616,256]{1,0:T(8,128)S(1)} %get-tuple-element.23.highs_ref), custom_call_target="tpu_custom_call" | custom-call | tf_op jit(solution)/shard_map/low_half/pallas_call | solution.py:351
  7.2 0.0 collective-permute-done.xin_ref
  7.2 0.1 edges.1
  7.3 3.2 %collective-permute-start.1 = (f32[48,128]{1,0:T(8,128)S(1)}, f32[48,128]{1,0:T(8,128)S(1)}, u32[]{:S(2)}, u32[]{:S(2)}) collective-permute-start(f32[48,128]{1,0:T(8,128)S(1)} %get-tuple-element.29), channel_id=1, source_target_pairs={{0,8},{8,16},{16,24},{24,32},{32,40},{40,48},{48,56},{56,0},{1,9},... | collective-permute-start | bytes 73736 | tf_op jit(solution)/shard_map/ppermute | solution.py:535
  10.5 1.6 %collective-permute-start.2 = (f32[32,128]{1,0:T(8,128)S(1)}, f32[32,128]{1,0:T(8,128)S(1)}, u32[]{:S(2)}, u32[]{:S(2)}) collective-permute-start(f32[32,128]{1,0:T(8,128)S(1)} %get-tuple-element.30), channel_id=1, source_target_pairs={{0,1},{1,2},{2,3},{3,4},{4,5},{5,6},{6,7},{7,0},{8,9},{9,10},{10,1... | collective-permute-start | bytes 49160 | tf_op jit(solution)/shard_map/ppermute | solution.py:535
  12.1 1.7 %collective-permute-start.3 = (f32[8,128]{1,0:T(8,128)S(1)}, f32[8,128]{1,0:T(8,128)S(1)}, u32[]{:S(2)}, u32[]{:S(2)}) collective-permute-start(f32[8,128]{1,0:T(8,128)S(1)} %get-tuple-element.31), channel_id=1, source_target_pairs={{0,9},{1,10},{2,11},{3,12},{4,13},{5,14},{6,15},{7,8},{8,17},{9,18... | collective-permute-start | bytes 12296 | tf_op jit(solution)/shard_map/ppermute | solution.py:535
  13.8 2.7 %collective-permute-done.3.yzin_ref = f32[8,128]{1,0:T(8,128)S(1)} collective-permute-done((f32[8,128]{1,0:T(8,128)S(1)}, f32[8,128]{1,0:T(8,128)S(1)}, u32[]{:S(2)}, u32[]{:S(2)}) %collective-permute-start.3) | collective-permute-done | bytes 4128 | tf_op jit(solution)/shard_map/ppermute | solution.py:535
  16.5 0.6 %collective-permute-done.2.zin_ref = f32[32,128]{1,0:T(8,128)S(1)} collective-permute-done((f32[32,128]{1,0:T(8,128)S(1)}, f32[32,128]{1,0:T(8,128)S(1)}, u32[]{:S(2)}, u32[]{:S(2)}) %collective-permute-start.2) | collective-permute-done | bytes 16416 | tf_op jit(solution)/shard_map/ppermute | solution.py:535
  17.2 0.0 collective-permute-done.1.yin_ref
  17.2 0.3 finish.1
  17.5 24.2 %all_to_all.11 = f32[256,1,128]{2,1,0:T(1,128)S(1)} all-to-all(f32[256,1,128]{2,1,0:T(1,128)S(1)} %bitcast.5), channel_id=1, replica_groups=mesh['gx'=4,'gy_0'=4,'gy_1'=2,'gz'=8] {'gx','gy_0','gy_1','gz'}, dimensions={0} | all-to-all | bytes 262144 | tf_op jit(solution)/shard_map/all_to_all | solution.py:548
  41.7 1.0 %scale.1 = (f32[32,32,128]{2,1,0:T(8,128)}, f32[16,16,64]{2,1,0:T(8,128)}, f32[8,8,32]{2,1,0:T(8,128)}, f32[4,4,16]{2,1,0:T(4,128)}, f32[2,2,8]{2,1,0:T(2,128)}, /*index=5*/f32[5]{0:T(128)}) custom-call(f32[256,128]{1,0:T(8,128)S(1)} %bitcast.4, f32[32,32,128]{2,1,0:T(8,128)S(1)} %get-tuple-element.33.refs_0_, f32[16,16,128]{2,1,0:T(8,128)S(1)} %get-tuple-element.34.refs_1_, ...), custom_call_target="tpu_custom_call" | custom-call | tf_op jit(solution)/shard_map/scale/pallas_call | solution.py:516
Async XLA Ops:
  2.5 4.6 %collective-permute-start = (f32[56,128]{1,0:T(8,128)S(1)}, f32[56,128]{1,0:T(8,128)S(1)}, u32[]{:S(2)}, u32[]{:S(2)}) collective-permute-start(f32[56,128]{1,0:T(8,128)S(1)} %get-tuple-element.26), channel_id=1, source_target_pairs={{0,64},{64,128},{128,192},{192,0},{1,65},{65,129},{129,193},{193,1... | collective-permute-start | bytes 86024 | tf_op jit(solution)/shard_map/ppermute | solution.py:535
  7.3 9.9 %collective-permute-start.1 = (f32[48,128]{1,0:T(8,128)S(1)}, f32[48,128]{1,0:T(8,128)S(1)}, u32[]{:S(2)}, u32[]{:S(2)}) collective-permute-start(f32[48,128]{1,0:T(8,128)S(1)} %get-tuple-element.29), channel_id=1, source_target_pairs={{0,8},{8,16},{16,24},{24,32},{32,40},{40,48},{48,56},{56,0},{1,9},... | collective-permute-start | bytes 73736 | tf_op jit(solution)/shard_map/ppermute | solution.py:535
  10.5 6.7 %collective-permute-start.2 = (f32[32,128]{1,0:T(8,128)S(1)}, f32[32,128]{1,0:T(8,128)S(1)}, u32[]{:S(2)}, u32[]{:S(2)}) collective-permute-start(f32[32,128]{1,0:T(8,128)S(1)} %get-tuple-element.30), channel_id=1, source_target_pairs={{0,1},{1,2},{2,3},{3,4},{4,5},{5,6},{6,7},{7,0},{8,9},{9,10},{10,1... | collective-permute-start | bytes 49160 | tf_op jit(solution)/shard_map/ppermute | solution.py:535
  12.1 4.4 %collective-permute-start.3 = (f32[8,128]{1,0:T(8,128)S(1)}, f32[8,128]{1,0:T(8,128)S(1)}, u32[]{:S(2)}, u32[]{:S(2)}) collective-permute-start(f32[8,128]{1,0:T(8,128)S(1)} %get-tuple-element.31), channel_id=1, source_target_pairs={{0,9},{1,10},{2,11},{3,12},{4,13},{5,14},{6,15},{7,8},{8,17},{9,18... | collective-permute-start | bytes 12296 | tf_op jit(solution)/shard_map/ppermute | solution.py:535
